TPU v7x, 256 devices: a whole 4x4x8 slice. The times are simulated.
256 devices in a mesh: dp: 4 (over x), expert: 64 (over y, z, core).
Axes of the slice: x: 4, y: 4, z: 8, core: 2. Of those that a mesh axis runs over, the one named last changes fastest.
Arguments:
- tokens: bfloat16 [32768, 2048], P(('dp', 'expert')), may hold values from -6 to 6
- cotangent: bfloat16 [32768, 2048], P(('dp', 'expert')), may hold values from -6 to 6
- routes: int32 [32768, 8], P(('dp', 'expert')), may hold values from 0 to 63, all different within a row; in each aligned block of 128 rows (0 to 127, 128 to 255, ...) at most 18 rows name the same one
- probs: bfloat16 [32768, 8], P(('dp', 'expert')), may hold values from 0.019897461 to 0.29882812
- slot_expert: int32 [64], replicated, may hold values from 0 to 63, each once
- gate_w: bfloat16 [64, 2048, 384], P('expert', 'dp'), may hold values from -0.125 to 0.125
- up_w: bfloat16 [64, 2048, 384], P('expert', 'dp'), may hold values from -0.125 to 0.125
- down_w: bfloat16 [64, 384, 2048], P('expert', None, 'dp'), may hold values from -0.3125 to 0.3125
Outputs:
- grad_tokens: bfloat16 [32768, 2048], P(('dp', 'expert'))
- grad_probs: bfloat16 [32768, 8], P(('dp', 'expert'))
- grad_gate: float32 [64, 2048, 384], P('expert', 'dp')
- grad_up: float32 [64, 2048, 384], P('expert', 'dp')
- grad_down: float32 [64, 384, 2048], P('expert', None, 'dp')
Inputs may be any that keep to these rules, and one draw needn't show every extreme that they name: `routes`: in each aligned block of 128 rows (the tokens of one device) no expert is named by more than 18 rows, a bound that some block reaches; a row names 8 different experts. `slot_expert`: each expert stands in exactly one slot.
All inputs are finite; a program needn't handle non-finite values.
Results may differ from a plain program's by a relative error of at most 0.008.
Values may be sent and summed in bfloat16 or wider, within the bound.
A program may use at most 128 MiB of HBM per device.

v0:
```python
import jax
import jax.numpy as jnp
from jax import lax
from jax.sharding import PartitionSpec as P

CAP = 18


def forward_part(got_x, w_gate, w_up):
    gate = jnp.einsum("sekd,edf->sekf", got_x, w_gate, preferred_element_type=jnp.float32)
    upval = jnp.einsum("sekd,edf->sekf", got_x, w_up, preferred_element_type=jnp.float32)
    sig = jax.nn.sigmoid(gate)
    act = gate * sig
    hidden = (act * upval).astype(jnp.bfloat16)
    return (gate, upval, sig, act, hidden)


def shards(tokens, cotangent, routes, probs, slot_expert, gate_w, up_w, down_w):
    n_exp = lax.axis_size("expert")
    local = gate_w.shape[0]
    tok_rows = tokens.shape[0]
    top = routes.shape[1]
    width = tokens.shape[1]
    count = local * n_exp
    rows_all = count * CAP
    flat = routes.reshape(-1)
    labels = jnp.arange(count, dtype=jnp.int32)
    match = slot_expert[None, :] == labels[:, None]
    slot_of = jnp.sum(jnp.where(match, labels[None, :], 0), axis=1)
    picked = flat[:, None] == labels[None, :]
    target = jnp.sum(jnp.where(picked, slot_of[None, :], 0), axis=1)
    hits = picked.astype(jnp.int32)
    position = jnp.sum((jnp.cumsum(hits, axis=0) - hits) * hits, axis=1)
    where_row = target * CAP + position
    placed = where_row[None, :] == jnp.arange(rows_all, dtype=jnp.int32)[:, None]
    token_map = jnp.any(placed.reshape(rows_all, tok_rows, top), axis=2).astype(jnp.bfloat16)
    send_x = jnp.dot(token_map, tokens, preferred_element_type=jnp.float32).astype(jnp.bfloat16)
    send_x = send_x.reshape(n_exp, local * CAP, width)
    send_dy = jnp.dot(token_map, cotangent, preferred_element_type=jnp.float32).astype(jnp.bfloat16)
    send_dy = send_dy.reshape(n_exp, local * CAP, width)
    zero_p = jnp.zeros((), jnp.bfloat16)
    send_p = jnp.sum(jnp.where(placed, probs.reshape(-1)[None, :], zero_p), axis=1).reshape(
        n_exp, local * CAP
    )
    w_gate, w_up, w_down = (
        lax.all_gather(gate_w, "dp", axis=1, tiled=True),
        lax.all_gather(up_w, "dp", axis=1, tiled=True),
        lax.all_gather(down_w, "dp", axis=2, tiled=True),
    )
    shape_rows = (n_exp, local, CAP, width)
    got_x = lax.all_to_all(send_x, "expert", split_axis=0, concat_axis=0, tiled=True).reshape(
        shape_rows
    )
    gate, upval, sig, act, hidden = forward_part(got_x, w_gate, w_up)
    got_dy, got_p = (
        lax.all_to_all(send_dy, "expert", split_axis=0, concat_axis=0, tiled=True),
        lax.all_to_all(send_p, "expert", split_axis=0, concat_axis=0, tiled=True),
    )
    got_dy = got_dy.reshape(shape_rows)
    weight = got_p.reshape(n_exp, local, CAP).astype(jnp.float32)[..., None]
    back = jnp.einsum("sekd,efd->sekf", got_dy, w_down, preferred_element_type=jnp.float32)
    dprob = jnp.sum(hidden.astype(jnp.float32) * back, axis=-1).astype(jnp.bfloat16)
    dh = weight * back
    d_gate = (dh * upval * sig * (1.0 + gate * (1.0 - sig))).astype(jnp.bfloat16)
    d_up = (dh * act).astype(jnp.bfloat16)
    dx_rows = (
        jnp.einsum("sekf,edf->sekd", d_gate, w_gate, preferred_element_type=jnp.float32)
        + jnp.einsum("sekf,edf->sekd", d_up, w_up, preferred_element_type=jnp.float32)
    ).astype(jnp.bfloat16)
    back_x, back_p = (
        lax.all_to_all(
            dx_rows.reshape(n_exp, local * CAP, width),
            "expert",
            split_axis=0,
            concat_axis=0,
            tiled=True,
        ),
        lax.all_to_all(
            dprob.reshape(n_exp, local * CAP), "expert", split_axis=0, concat_axis=0, tiled=True
        ),
    )
    wdy = (weight * got_dy.astype(jnp.float32)).astype(jnp.bfloat16)
    part_gate = jnp.einsum("sekd,sekf->edf", got_x, d_gate, preferred_element_type=jnp.float32)
    part_up = jnp.einsum("sekd,sekf->edf", got_x, d_up, preferred_element_type=jnp.float32)
    part_down = jnp.einsum("sekf,sekd->efd", hidden, wdy, preferred_element_type=jnp.float32)
    grad_gate, grad_up, grad_down = (
        lax.psum_scatter(part_gate, "dp", scatter_dimension=1, tiled=True),
        lax.psum_scatter(part_up, "dp", scatter_dimension=1, tiled=True),
        lax.psum_scatter(part_down, "dp", scatter_dimension=2, tiled=True),
    )
    returned_rows = back_x.reshape(rows_all, width)
    grad_tokens = lax.dot_general(
        token_map, returned_rows, (((0,), (0,)), ((), ())), preferred_element_type=jnp.float32
    ).astype(jnp.bfloat16)
    grad_probs = jnp.sum(jnp.where(placed, back_p.reshape(rows_all)[:, None], zero_p), axis=0)
    grad_probs = grad_probs.reshape(tok_rows, top)
    return (grad_tokens, grad_probs, grad_gate, grad_up, grad_down)


def solution(mesh):
    placed = (
        P(("dp", "expert"), None),
        P(("dp", "expert"), None),
        P(("dp", "expert"), None),
        P(("dp", "expert"), None),
        P(),
        P("expert", "dp", None),
        P("expert", "dp", None),
        P("expert", None, "dp"),
    )
    return jax.shard_map(
        shards,
        mesh=mesh,
        in_specs=placed,
        out_specs=(
            P(("dp", "expert"), None),
            P(("dp", "expert"), None),
            P("expert", "dp", None),
            P("expert", "dp", None),
            P("expert", None, "dp"),
        ),
        check_vma=False,
    )
```

profile of v0, /device:TPU:32, one launch (start us, length us, event | category | flops | bytes accessed | tf_op | source)
XLA Modules:
  0.0 582.6 jit_solution(18308793339470414094)
XLA Ops:
  7.2 0.0 copy-start
  7.2 0.8 copy.42
  8.0 0.1 eq.65
  8.1 0.1 eq.58
  8.2 0.8 select_reduce_fusion.1
  9.0 18.0 %reduce-window.6 = s32[64,8,128]{2,1,0:T(8,128)S(1)} reduce-window(s32[64,8,128]{2,1,0:T(8,128)S(1)} %fusion.40, s32[]{:T(128)} %constant.6.clone.1), window={size=1x1x128 pad=0_0x0_0x127_0}, to_apply=%region_2.3 | reduce-window | flops 8323072 | bytes 524292 | tf_op jit(solution)/shard_map/reduce-window
  27.0 0.1 slice.8
  27.2 0.1 copy.44
  27.3 0.1 copy.45
  27.4 0.1 broadcast_add_fusion
  27.6 0.1 select_reduce_fusion
  27.7 0.1 add.30
  27.8 4.2 fusion.6
  32.1 3.5 convolution_convert_fusion
  35.6 7.6 %reshape.142 = bf16[64,18,2048]{2,1,0:T(8,128)(2,1)} reshape(bf16[1152,2048]{1,0:T(8,128)(2,1)} %convolution_convert_fusion) | data formatting | bytes 9437184 | tf_op jit(solution)/shard_map/reshape | solution.py:38
  43.1 12.1 %all-to-all-start.2 = ((bf16[64,18,2048]{2,1,0:T(8,128)(2,1)}), bf16[64,18,2048]{2,1,0:T(8,128)(2,1)}, u32[]{:S(2)}, u32[]{:S(2)}) async-start(bf16[64,18,2048]{2,1,0:T(8,128)(2,1)} %reshape.142), calls=%async_computation.2 | async-start | bytes 12582912 | tf_op jit(solution)/shard_map/all_to_all | solution.py:51
  55.2 3.5 convolution_convert_fusion.1
  58.7 7.6 %reshape.140 = bf16[64,18,2048]{2,1,0:T(8,128)(2,1)} reshape(bf16[1152,2048]{1,0:T(8,128)(2,1)} %convolution_convert_fusion.1) | data formatting | bytes 9437184 | tf_op jit(solution)/shard_map/reshape | solution.py:40
  66.3 127.8 %all-to-all-done.2 = bf16[64,18,2048]{2,1,0:T(8,128)(2,1)} async-done(((bf16[64,18,2048]{2,1,0:T(8,128)(2,1)}), bf16[64,18,2048]{2,1,0:T(8,128)(2,1)}, u32[]{:S(2)}, u32[]{:S(2)}) %all-to-all-start.2) | async-done | bytes 4718624 | tf_op jit(solution)/shard_map/all_to_all | solution.py:51
  194.1 7.9 %all-to-all-start.1 = ((bf16[64,18,2048]{2,1,0:T(8,128)(2,1)}), bf16[64,18,2048]{2,1,0:T(8,128)(2,1)}, u32[]{:S(2)}, u32[]{:S(2)}) async-start(bf16[64,18,2048]{2,1,0:T(8,128)(2,1)} %reshape.140), calls=%async_computation.1 | async-start | bytes 12582912 | tf_op jit(solution)/shard_map/all_to_all | solution.py:56
  202.0 0.0 all-gather.8.cloned.1.call-start
  202.0 0.7 all-gather.8.cloned.1.call-update
  202.7 0.0 all-gather.6.cloned.1.call-start
  202.8 0.7 all-gather.6.cloned.1.call-update
  203.5 0.2 all-gather.4.cloned.1.call-start
  203.7 0.5 all-gather.4.cloned.1.call-update
  204.2 30.6 %all-gather.8.cloned.1.call-done = bf16[1,2048,384]{2,1,0:T(8,128)(2,1)} async-done(((bf16[1,512,384]{2,1,0:T(8,128)(2,1)}), bf16[1,2048,384]{2,1,0:T(8,128)(2,1)}) %all-gather.8.cloned.1.call-update) | async-done | bytes 1572880 | tf_op jit(solution)/shard_map/all_gather | solution.py:46
  234.8 7.9 %fusion.23 = f32[64,18,384]{2,0,1:T(8,128)S(1)} fusion(bf16[1,2048,384]{2,1,0:T(8,128)(2,1)} %all-gather.8.cloned.1.call-done, bf16[64,18,2048]{2,1,0:T(8,128)(2,1)} %all-to-all-done.2), kind=kOutput, calls=%fused_computation.38 | convolution fusion | flops 1811939328 | bytes 8060928 | tf_op jit(solution)/shard_map/sekd,edf->sekf/dot_general | solution.py:10
  242.7 22.9 %all-gather.6.cloned.1.call-done = bf16[1,2048,384]{2,1,0:T(8,128)(2,1)} async-done(((bf16[1,512,384]{2,1,0:T(8,128)(2,1)}), bf16[1,2048,384]{2,1,0:T(8,128)(2,1)}) %all-gather.6.cloned.1.call-update) | async-done | bytes 1572880 | tf_op jit(solution)/shard_map/all_gather | solution.py:47
  265.6 7.6 %fusion.26 = f32[64,18,384]{2,0,1:T(8,128)} fusion(bf16[1,2048,384]{2,1,0:T(8,128)(2,1)} %all-gather.6.cloned.1.call-done, bf16[64,18,2048]{2,1,0:T(8,128)(2,1)} %all-to-all-done.2), kind=kOutput, calls=%fused_computation.41 | convolution fusion | flops 1811939328 | bytes 8060928 | tf_op jit(solution)/shard_map/sekd,edf->sekf/dot_general | solution.py:11
  273.3 23.2 %all-gather.4.cloned.1.call-done = bf16[1,384,2048]{2,1,0:T(8,128)(2,1)} async-done(((bf16[1,384,512]{2,1,0:T(8,128)(2,1)}), bf16[1,384,2048]{2,1,0:T(8,128)(2,1)}) %all-gather.4.cloned.1.call-update) | async-done | bytes 1572880 | tf_op jit(solution)/shard_map/all_gather | solution.py:48
  296.5 44.4 %all-to-all-done.1 = bf16[64,18,2048]{2,1,0:T(8,128)(2,1)} async-done(((bf16[64,18,2048]{2,1,0:T(8,128)(2,1)}), bf16[64,18,2048]{2,1,0:T(8,128)(2,1)}, u32[]{:S(2)}, u32[]{:S(2)}) %all-to-all-start.1) | async-done | bytes 4718624 | tf_op jit(solution)/shard_map/all_to_all | solution.py:56
  340.9 8.4 %fusion.12 = (bf16[64,18]{0,1:T(8,128)(2,1)S(1)}, bf16[64,1,18,384]{3,0,2,1:T(8,128)(2,1)S(1)}, f32[64,18,384]{2,0,1:T(8,128)}) fusion(f32[64,18,384]{2,0,1:T(8,128)} %fusion.26, f32[64,18,384]{2,0,1:T(8,128)S(1)} %fusion.23, bf16[1,384,2048]{2,1,0:T(8,128)(2,1)} %all-gather.4.cloned.1.call-done, bf16[64,18,2048]{2,1,0:T(8,128)(2,1)} %all-to-all-done.1), kind=kOutput, calls=%fused_computation.21 | convolution fusion | flops 1815919488 | bytes 12486912 | tf_op jit(solution)/shard_map/sekd,efd->sekf/dot_general | solution.py:61
  349.3 0.7 copy.54
  350.0 7.7 %all-to-all-start.4 = ((bf16[64,1,18]{2,1,0:T(2,128)(2,1)}), bf16[64,1,18]{2,1,0:T(2,128)(2,1)S(1)}, u32[]{:S(2)}, u32[]{:S(2)}) async-start(bf16[64,1,18]{2,1,0:T(2,128)(2,1)} %copy.54), calls=%async_computation.4 | async-start | bytes 65536 | tf_op jit(solution)/shard_map/all_to_all | solution.py:78
  357.8 0.0 reduce-scatter.8.cloned.1.call-start
  357.8 0.1 copy.47
  357.9 0.1 broadcast_in_dim.62
  358.1 8.2 %all-to-all-done.4 = bf16[64,1,18]{2,1,0:T(2,128)(2,1)S(1)} async-done(((bf16[64,1,18]{2,1,0:T(2,128)(2,1)}), bf16[64,1,18]{2,1,0:T(2,128)(2,1)S(1)}, u32[]{:S(2)}, u32[]{:S(2)}) %all-to-all-start.4) | async-done | bytes 2336 | tf_op jit(solution)/shard_map/all_to_all | solution.py:78
  366.3 0.1 reduce.3
  366.4 0.1 broadcast_in_dim.65
  366.5 1.2 fusion.11
  367.7 0.2 all_to_all.25
  367.8 13.5 %all_to_all.31 = bf16[64,1,18]{2,1,0:T(2,128)(2,1)S(1)} all-to-all(bf16[64,1,18]{2,1,0:T(2,128)(2,1)S(1)} %all_to_all.25), channel_id=1, replica_groups=mesh['dp'=4,'expert'=64] {'expert'}, dimensions={0} | all-to-all | bytes 4608 | tf_op jit(solution)/shard_map/all_to_all | solution.py:57
  381.4 3.9 multiply_convert_fusion
  385.3 7.9 %fusion.7 = f32[1,384,2048]{2,1,0:T(8,128)} fusion(bf16[64,18,2048]{2,1,0:T(8,128)(2,1)S(1)} %multiply_convert_fusion, bf16[64,1,18,384]{3,0,2,1:T(8,128)(2,1)S(1)} %get-tuple-element.25), kind=kOutput, calls=%fused_computation.13 | convolution fusion | flops 1811939328 | bytes 8749056 | tf_op jit(solution)/shard_map/sekf,sekd->efd/dot_general | solution.py:85
  393.2 0.0 reduce-scatter.8.cloned.1.call-update
  393.2 0.4 reduce-scatter.4.cloned.1.call-start
  393.7 0.1 copy.49
  393.7 3.4 fusion.29
  397.2 8.4 %convolution_bitcast_fusion.1 = f32[1,2048,384]{2,1,0:T(8,128)} fusion(bf16[64,1,18,384]{3,0,2,1:T(8,128)(2,1)S(1)} %get-tuple-element.27, bf16[64,18,2048]{2,1,0:T(8,128)(2,1)} %all-to-all-done.2), kind=kOutput, calls=%fused_computation.15 | convolution fusion | flops 1811939328 | bytes 8749056 | tf_op jit(solution)/shard_map/sekd,sekf->edf/dot_general | solution.py:83
  405.6 0.0 reduce-scatter.4.cloned.1.call-update
  405.7 4.2 fusion.21
  409.8 2.9 add_convert_fusion
  412.7 5.4 copy.53
  418.1 6.7 %all-to-all-start.3 = ((bf16[64,18,2048]{2,1,0:T(8,128)(2,1)}), bf16[64,18,2048]{2,1,0:T(8,128)(2,1)}, u32[]{:S(2)}, u32[]{:S(2)}) async-start(bf16[64,18,2048]{2,1,0:T(8,128)(2,1)} %copy.53), calls=%async_computation.3 | async-start | bytes 12582912 | tf_op jit(solution)/shard_map/all_to_all | solution.py:71
  424.8 0.2 reduce-scatter.6.cloned.1.call-start
  425.1 8.6 %convolution_bitcast_fusion = f32[1,2048,384]{2,1,0:T(8,128)} fusion(bf16[64,18,384]{2,0,1:T(8,128)(2,1)S(1)} %get-tuple-element.26, bf16[64,18,2048]{2,1,0:T(8,128)(2,1)} %all-to-all-done.2), kind=kOutput, calls=%fused_computation.14 | convolution fusion | flops 1811939328 | bytes 8749056 | tf_op jit(solution)/shard_map/sekd,sekf->edf/dot_general | solution.py:84
  433.6 0.0 reduce-scatter.6.cloned.1.call-update
  433.7 0.1 reshape.148
  433.8 0.7 copy.58
  434.4 129.3 %all-to-all-done.3 = bf16[64,18,2048]{2,1,0:T(8,128)(2,1)} async-done(((bf16[64,18,2048]{2,1,0:T(8,128)(2,1)}), bf16[64,18,2048]{2,1,0:T(8,128)(2,1)}, u32[]{:S(2)}, u32[]{:S(2)}) %all-to-all-start.3) | async-done | bytes 4718624 | tf_op jit(solution)/shard_map/all_to_all | solution.py:71
  563.8 7.8 %reshape.147 = bf16[1152,2048]{1,0:T(8,128)(2,1)} reshape(bf16[64,18,2048]{2,1,0:T(8,128)(2,1)} %all-to-all-done.3) | data formatting | bytes 9437184 | tf_op jit(solution)/shard_map/reshape | solution.py:91
  571.5 4.0 convolution_convert_fusion.2
  (20 shorter events, 0.2 us)
Async XLA Ops:
  7.2 24.9 %copy-start = (bf16[128,2048]{1,0:T(8,128)(2,1)S(1)}, bf16[128,2048]{1,0:T(8,128)(2,1)}, u32[]{:S(2)}) copy-start(bf16[128,2048]{1,0:T(8,128)(2,1)} %param.8) | copy-start | bytes 1572868
  43.1 12.1 %copy-start.4 = (bf16[128,2048]{1,0:T(8,128)(2,1)S(1)}, bf16[128,2048]{1,0:T(8,128)(2,1)}, u32[]{:S(2)}) copy-start(bf16[128,2048]{1,0:T(8,128)(2,1)} %param.9) | copy-start | bytes 1572868
  43.1 151.0 %all-to-all-start.2 = ((bf16[64,18,2048]{2,1,0:T(8,128)(2,1)}), bf16[64,18,2048]{2,1,0:T(8,128)(2,1)}, u32[]{:S(2)}, u32[]{:S(2)}) async-start(bf16[64,18,2048]{2,1,0:T(8,128)(2,1)} %reshape.142), calls=%async_computation.2 | async-start | bytes 12582912 | tf_op jit(solution)/shard_map/all_to_all | solution.py:51
  194.1 146.8 %all-to-all-start.1 = ((bf16[64,18,2048]{2,1,0:T(8,128)(2,1)}), bf16[64,18,2048]{2,1,0:T(8,128)(2,1)}, u32[]{:S(2)}, u32[]{:S(2)}) async-start(bf16[64,18,2048]{2,1,0:T(8,128)(2,1)} %reshape.140), calls=%async_computation.1 | async-start | bytes 12582912 | tf_op jit(solution)/shard_map/all_to_all | solution.py:56
  202.0 32.8 %all-gather.8.cloned.1.call-start = ((), (), s32[]{:S(2)}) async-start(), calls=%async_computation.10 | async-start | bytes 1966080 | tf_op jit(solution)/shard_map/all_gather | solution.py:46
  202.7 62.9 %all-gather.6.cloned.1.call-start = ((), (), s32[]{:S(2)}) async-start(), calls=%async_computation.9 | async-start | bytes 1966080 | tf_op jit(solution)/shard_map/all_gather | solution.py:47
  203.5 93.0 %all-gather.4.cloned.1.call-start = ((), (), s32[]{:S(2)}) async-start(), calls=%async_computation.8 | async-start | bytes 1966080 | tf_op jit(solution)/shard_map/all_gather | solution.py:48
  242.7 98.2 %copy-start.2 = (f32[64,18,384]{2,0,1:T(8,128)}, f32[64,18,384]{2,0,1:T(8,128)S(1)}, u32[]{:S(2)}) copy-start(f32[64,18,384]{2,0,1:T(8,128)S(1)} %fusion.23) | copy-start | bytes 5308420
  273.3 84.6 %copy-start.5 = (bf16[128,8]{0,1:T(8,128)(2,1)S(1)}, bf16[128,8]{0,1:T(8,128)(2,1)}, u32[]{:S(2)}) copy-start(bf16[128,8]{0,1:T(8,128)(2,1)} %param.11) | copy-start | bytes 6148
  350.0 16.2 %all-to-all-start.4 = ((bf16[64,1,18]{2,1,0:T(2,128)(2,1)}), bf16[64,1,18]{2,1,0:T(2,128)(2,1)S(1)}, u32[]{:S(2)}, u32[]{:S(2)}) async-start(bf16[64,1,18]{2,1,0:T(2,128)(2,1)} %copy.54), calls=%async_computation.4 | async-start | bytes 65536 | tf_op jit(solution)/shard_map/all_to_all | solution.py:78
  357.8 217.8 %reduce-scatter.8.cloned.1.call-start = ((), (), s32[]{:S(2)}) async-start(), calls=%async_computation.13 | async-start | bytes 3932160 | tf_op jit(solution)/shard_map/reduce_scatter | solution.py:89
  393.2 182.4 %reduce-scatter.4.cloned.1.call-start = ((), (), s32[]{:S(2)}) async-start(), calls=%async_computation.11 | async-start | bytes 3932160 | tf_op jit(solution)/shard_map/reduce_scatter | solution.py:87
  405.6 4.2 copy-start.3
  418.1 145.6 %all-to-all-start.3 = ((bf16[64,18,2048]{2,1,0:T(8,128)(2,1)}), bf16[64,18,2048]{2,1,0:T(8,128)(2,1)}, u32[]{:S(2)}, u32[]{:S(2)}) async-start(bf16[64,18,2048]{2,1,0:T(8,128)(2,1)} %copy.53), calls=%async_computation.3 | async-start | bytes 12582912 | tf_op jit(solution)/shard_map/all_to_all | solution.py:71
  424.8 150.7 %reduce-scatter.6.cloned.1.call-start = ((), (), s32[]{:S(2)}) async-start(), calls=%async_computation.12 | async-start | bytes 3932160 | tf_op jit(solution)/shard_map/reduce_scatter | solution.py:88
  563.8 11.8 %copy-start.1 = (bf16[128,2048]{1,0:T(8,128)(2,1)S(1)}, bf16[128,2048]{1,0:T(8,128)(2,1)}, u32[]{:S(2)}) copy-start(bf16[128,2048]{1,0:T(8,128)(2,1)} %param.8) | copy-start | bytes 1572868
Sparse Core Ops, SparseCore 0:
  204.6 30.1 all-gather.7
  236.6 28.9 all-gather.5
  267.4 28.9 all-gather.3
  393.3 36.4 reduce-scatter.7
  432.8 40.5 reduce-scatter.3
  476.4 40.5 reduce-scatter.5
where the time goes:
time: 593 us; the launch traced here: 583 us
  waiting for transfers between devices  388 us (65%)
  matrix products  67 us (11%)
  starting transfers between devices  35.4 us (6%)
  local copies, waits for them, and re-layouts  31.9 us (5%)
  other arithmetic  31.9 us (5%)
  between operations  14.5 us (2%)
  blocking collectives  13.5 us (2%)
    all_to_all x1, waiting for transfers between devices, shards(): lax.all_to_all(dx_rows.reshape(n_exp, local * CAP, width), 'expert', spli...  129 us
    all_to_all x1, waiting for transfers between devices, shards(): lax.all_to_all(send_x, 'expert', split_axis=0, concat_axis=0, tiled=True)  128 us
    all_to_all x1, waiting for transfers between devices, shards(): lax.all_to_all(send_dy, 'expert', split_axis=0, concat_axis=0, tiled=True)  44.4 us
    all_gather x1, waiting for transfers between devices, shards(): lax.all_gather(gate_w, 'dp', axis=1, tiled=True)  30.6 us
    all_gather x1, waiting for transfers between devices, shards(): lax.all_gather(down_w, 'dp', axis=2, tiled=True)  23.2 us
    all_gather x1, waiting for transfers between devices, shards(): lax.all_gather(up_w, 'dp', axis=1, tiled=True)  22.9 us
    another operation x4, other arithmetic  21.6 us
    all_to_all x1, blocking collectives, shards(): lax.all_to_all(send_p, 'expert', split_axis=0, concat_axis=0, tiled=True)  13.5 us
  transfers between devices with their start and end apart: 10, of which 7 were waited for; matrix products, arithmetic and copies ran while one was open for 12% of the time, Pallas kernels for 0%

commit v1 on v0

v1 whole, which is shorter than its diff:
```python
import functools

import jax
import jax.numpy as jnp
from jax import lax
from jax.experimental import pallas as pl
from jax.experimental.pallas import tpu as pltpu
from jax.sharding import PartitionSpec as P

CAP = 18
NX, NY, NZ, NC = 4, 4, 8, 2
PLANE = NY * NC
ROWS = NZ * CAP
MESH = pl.DeviceIdType.MESH
F32 = jnp.float32
BF16 = jnp.bfloat16


def mod(a, n):
    return lax.rem(a + n, n)


class Place:
    def __init__(self):
        self.x = lax.axis_index("dp")
        e = lax.axis_index("expert")
        self.c = lax.rem(e, NC)
        self.z = lax.rem(lax.div(e, NC), NZ)
        self.y = lax.div(e, NC * NZ)
        self.plane = self.y * NC + self.c

    def dev(self, y, z, c):
        return {"expert": (y * NZ + z) * NC + c}

    def at_z(self, step):
        return self.dev(self.y, mod(self.z + step, NZ), self.c)

    def at_y(self, step, c):
        return self.dev(mod(self.y + step, NY), self.z, c)

    def at_x(self, step):
        return {"dp": mod(self.x + step, NX)}

    def peers(self):
        out = [self.at_z(s) for s in range(1, NZ)]
        out += [self.at_y(s, c) for s in (1, -1) for c in range(NC)]
        out += [self.at_y(0, 1 - self.c), self.at_x(1), self.at_x(-1)]
        return out


def greet(me):
    barrier = pltpu.get_barrier_semaphore()
    peers = me.peers()
    for peer in peers:
        pl.semaphore_signal(barrier, inc=1, device_id=peer, device_id_type=MESH)
    pl.semaphore_wait(barrier, len(peers))


def remote(src, dst, send, recv, dev):
    return pltpu.make_async_remote_copy(
        src_ref=src, dst_ref=dst, send_sem=send, recv_sem=recv, device_id=dev, device_id_type=MESH
    )


def plane_send(me, piece, landing, relay, send, recv, relay_recv):
    for step, core in ((1, 0), (-1, 1)):
        remote(
            piece(mod(me.y + 2, NY) * NC + core), relay(core), send, relay_recv(core), me.at_y(step, me.c)
        ).start()
    for step in (1, -1):
        for core in range(NC):
            there = mod(me.y + step, NY)
            remote(piece(there * NC + core), landing(me.plane), send, recv, me.at_y(step, core)).start()
    remote(piece(me.y * NC + 1 - me.c), landing(me.plane), send, recv, me.at_y(0, 1 - me.c)).start()


def plane_relay(me, landing, relay, send, recv, relay_recv):
    for step, core in ((1, 0), (-1, 1)):
        remote(relay(core), relay(core), send, relay_recv(core), me.at_y(step, core)).wait_recv()
        origin = mod(me.y - step, NY) * NC + me.c
        remote(relay(core), landing(origin), send, recv, me.at_y(step, core)).start()


def dispatch_kernel(
    width,
    chunks,
    tok,
    cot,
    routes,
    probs,
    slots,
    gate,
    up,
    down,
    out_x,
    out_dy,
    out_p,
    all_gate,
    all_up,
    all_down,
    key_out,
    zbuf,
    sbuf,
    relay,
    maps_own,
    maps,
    pick,
    pbuf,
    prelay,
    own_sem,
    map_send,
    map_recv,
    z_send,
    z_recv,
    y_send,
    y_recv,
    r_recv,
    y_own,
    w_send,
    w_recv,
    w_own,
):
    me = Place()
    cw = width // chunks
    half = cw // 2
    total = 2 * chunks
    rows = tok.shape[0]

    def own_copy(k):
        src = (tok, cot)[k // chunks]
        return pltpu.make_async_copy(
            src.at[:, pl.ds((k % chunks) * cw, cw)], zbuf.at[k, me.z], own_sem.at[k]
        )

    for k in range(total):
        own_copy(k).start()

    hit = jnp.zeros((NZ * PLANE, rows), F32)
    weight = jnp.zeros((NZ * PLANE, rows), F32)
    named = slots[...]
    for k in range(routes.shape[0]):
        same = named == routes[k : k + 1, :]
        hit = hit + jnp.where(same, 1.0, 0.0)
        weight = weight + jnp.where(same, probs[k : k + 1, :], 0.0)
    before = lax.broadcasted_iota(jnp.int32, (rows, rows), 0) < lax.broadcasted_iota(
        jnp.int32, (rows, rows), 1
    )
    rank = jnp.dot(
        hit.astype(BF16), jnp.where(before, 1.0, 0.0).astype(BF16), preferred_element_type=F32
    )
    row_of = jnp.where(hit > 0.5, rank + (me.z * CAP).astype(F32), -1.0)
    for z in range(NZ):
        maps_own[z, 0] = row_of[z * PLANE : (z + 1) * PLANE]
        maps_own[z, 1] = weight[z * PLANE : (z + 1) * PLANE]
    maps[me.z] = maps_own[me.z]
    for k in range(total):
        own_copy(k).wait()

    greet(me)

    def z_copy(k, direction, stage):
        sign = 1 - 2 * direction
        block = mod(me.z - sign * stage, NZ)
        if stage == 3:
            where = zbuf.at[k, block, :, pl.ds(direction * half, half)]
        else:
            where = zbuf.at[k, block]
        return remote(
            where, where, z_send.at[k, direction, stage], z_recv.at[k, direction, stage], me.at_z(sign)
        )

    def z_wait(k, direction, stage):
        sign = 1 - 2 * direction
        block = mod(me.z - sign * (stage + 1), NZ)
        if stage == 3:
            where = zbuf.at[k, block, :, pl.ds(direction * half, half)]
        else:
            where = zbuf.at[k, block]
        remote(
            where, where, z_send.at[k, direction, stage], z_recv.at[k, direction, stage], me.at_z(sign)
        ).wait_recv()

    def z_stage(k, stage):
        for direction in (0, 1):
            if stage > 0:
                z_wait(k, direction, stage - 1)
            if stage < 4:
                z_copy(k, direction, stage).start()

    weights = ((gate, all_gate, True), (up, all_up, True), (down, all_down, False))

    def w_slot(n, owner):
        src, dst, lead = weights[n]
        if lead:
            return dst.at[owner]
        return dst.at[:, pl.ds(pl.multiple_of(owner * src.shape[1], 128), src.shape[1])]

    def w_copy(n, direction, hop):
        sign = 1 - 2 * direction
        owner = me.x if hop == 0 else mod(me.x - sign, NX)
        src = weights[n][0] if hop == 0 else w_slot(n, owner)
        return remote(
            src, w_slot(n, owner), w_send.at[n, direction, hop], w_recv.at[n, direction, hop], me.at_x(sign)
        )

    def w_wait(n, direction, hop):
        sign = 1 - 2 * direction
        slot = w_slot(n, mod(me.x - sign * (hop + 1), NX))
        remote(
            slot, slot, w_send.at[n, direction, hop], w_recv.at[n, direction, hop], me.at_x(sign)
        ).wait_recv()

    for s in range(1, NZ):
        z = mod(me.z + s, NZ)
        remote(maps_own.at[z], maps.at[me.z], map_send.at[s], map_recv.at[s], me.at_z(s)).start()
    z_stage(0, 0)
    for n in range(3):
        for direction in (0, 1):
            w_copy(n, direction, 0).start()
        pltpu.make_async_copy(weights[n][0], w_slot(n, me.x), w_own.at[n]).start()

    for s in range(1, NZ):
        z = mod(me.z - s, NZ)
        remote(maps.at[z], maps.at[z], map_send.at[s], map_recv.at[s], me.at_z(s)).wait_recv()
    row = lax.broadcasted_iota(jnp.int32, (ROWS, rows), 0).astype(F32)
    ones = jnp.ones((rows, rows), BF16)
    for d in range(PLANE):
        share = jnp.zeros((ROWS, rows), F32)
        for z in range(NZ):
            taken = maps[z, 0, d : d + 1, :] == row
            pick[d * ROWS : (d + 1) * ROWS, z * rows : (z + 1) * rows] = jnp.where(taken, 1.0, 0.0).astype(BF16)
            share = share + jnp.where(taken, maps[z, 1, d : d + 1, :], 0.0)
            key_out[d : d + 1, z * rows : (z + 1) * rows] = maps[z, 0, d : d + 1, :]
        pbuf[d] = jnp.dot(share.astype(BF16), ones, preferred_element_type=F32).astype(BF16)

    last = total

    def piece(k):
        return lambda d: sbuf.at[k, d]

    def relay_of(k):
        return lambda core: relay.at[k, core]

    def relay_sem(k):
        return lambda core: r_recv.at[k, core]

    def landing(k, out):
        col = pl.multiple_of(lax.rem(k, chunks) * cw, cw)
        return lambda slot: out.at[slot, :, pl.ds(col, cw)]

    def by_array(k, act):
        @pl.when(k < chunks)
        def _():
            act(out_x)

        @pl.when(k >= chunks)
        def _():
            act(out_dy)

    def send_chunk(k):
        def act(out):
            plane_send(
                me, piece(k), landing(k, out), relay_of(k), y_send.at[k], y_recv.at[k], relay_sem(k)
            )
            pltpu.make_async_copy(
                sbuf.at[k, me.plane], landing(k, out)(me.plane), y_own.at[k]
            ).start()

        by_array(k, act)

    def relay_chunk(k):
        by_array(
            k,
            lambda out: plane_relay(
                me, landing(k, out), relay_of(k), y_send.at[k], y_recv.at[k], relay_sem(k)
            ),
        )

    def p_land(slot):
        return out_p.at[slot]

    def p_relay(core):
        return prelay.at[core]

    def p_sem(core):
        return r_recv.at[last, core]

    def step(i, carry):
        @pl.when((i >= 1) & (i < total))
        def _():
            z_stage(i, 0)

        @pl.when((i >= 1) & (i <= total))
        def _():
            z_stage(i - 1, 2)

        @pl.when((i >= 2) & (i <= total + 1))
        def _():
            k = i - 2
            z_stage(k, 4)
            block = zbuf[k].reshape(NZ * rows, cw)
            out = jnp.dot(pick[...], block, preferred_element_type=F32).astype(BF16)
            sbuf[k] = out.reshape(PLANE, ROWS, cw)
            send_chunk(k)

        @pl.when(i < total)
        def _():
            z_stage(i, 1)

        @pl.when((i >= 1) & (i <= total))
        def _():
            z_stage(i - 1, 3)

        @pl.when((i >= 3) & (i <= total + 2))
        def _():
            relay_chunk(i - 3)

        @pl.when(i == 1)
        def _():
            for n in range(3):
                for direction in (0, 1):
                    w_wait(n, direction, 0)
                w_copy(n, 0 if n < 2 else 1, 1).start()

        @pl.when(i == 2)
        def _():
            plane_send(me, lambda d: pbuf.at[d], p_land, p_relay, y_send.at[last], y_recv.at[last], p_sem)
            pltpu.make_async_copy(pbuf.at[me.plane], out_p.at[me.plane], y_own.at[last]).start()

        @pl.when(i == 3)
        def _():
            plane_relay(me, p_land, p_relay, y_send.at[last], y_recv.at[last], p_sem)

        return carry

    lax.fori_loop(0, total + 3, step, 0)

    for n in range(3):
        w_wait(n, 0 if n < 2 else 1, 1)
        for direction in (0, 1):
            w_copy(n, direction, 0).wait_send()
        w_copy(n, 0 if n < 2 else 1, 1).wait_send()
        pltpu.make_async_copy(weights[n][0], w_slot(n, me.x), w_own.at[n]).wait()
    for s in range(1, NZ):
        z = mod(me.z + s, NZ)
        remote(maps_own.at[z], maps.at[me.z], map_send.at[s], map_recv.at[s], me.at_z(s)).wait_send()

    def drain(k, carry):
        for direction in (0, 1):
            for stage in range(4):
                z_copy(k, direction, stage).wait_send()

        def act(out):
            here = out.at[pl.ds(0, PLANE - 1), :, pl.ds(pl.multiple_of(lax.rem(k, chunks) * cw, cw), cw)]
            sent = sbuf.at[k, pl.ds(0, PLANE - 1)]
            remote(sent, here, y_send.at[k], y_recv.at[k], me.at_y(1, 0)).wait_recv()
            remote(sent, here, y_send.at[k], y_recv.at[k], me.at_y(1, 0)).wait_send()
            two = sbuf.at[k, pl.ds(0, 2)]
            remote(two, two, y_send.at[k], y_recv.at[k], me.at_y(1, 0)).wait_send()
            pltpu.make_async_copy(
                sbuf.at[k, me.plane], landing(k, out)(me.plane), y_own.at[k]
            ).wait()

        by_array(k, act)
        return carry

    lax.fori_loop(0, total, drain, 0)
    here, sent, two = out_p.at[pl.ds(0, PLANE - 1)], pbuf.at[pl.ds(0, PLANE - 1)], pbuf.at[pl.ds(0, 2)]
    remote(sent, here, y_send.at[last], y_recv.at[last], me.at_y(1, 0)).wait_recv()
    remote(sent, here, y_send.at[last], y_recv.at[last], me.at_y(1, 0)).wait_send()
    remote(two, two, y_send.at[last], y_recv.at[last], me.at_y(1, 0)).wait_send()
    pltpu.make_async_copy(pbuf.at[me.plane], out_p.at[me.plane], y_own.at[last]).wait()


def dispatch(tokens, cotangent, routes, probs, slots, gate, up, down, chunks=4):
    rows, width = tokens.shape
    depth, ff = gate.shape
    cw, total = width // chunks, 2 * chunks
    dma = pltpu.SemaphoreType.DMA
    vmem = pl.BlockSpec(memory_space=pltpu.VMEM)
    anyp = pl.BlockSpec(memory_space=pl.ANY)
    shape = jax.ShapeDtypeStruct
    return pl.pallas_call(
        functools.partial(dispatch_kernel, width, chunks),
        out_shape=(
            shape((PLANE, ROWS, width), BF16),
            shape((PLANE, ROWS, width), BF16),
            shape((PLANE, ROWS, rows), BF16),
            shape((NX, depth, ff), BF16),
            shape((NX, depth, ff), BF16),
            shape((ff, width), BF16),
            shape((PLANE, NZ * rows), F32),
        ),
        in_specs=[anyp, anyp, vmem, vmem, vmem, vmem, vmem, vmem],
        out_specs=(anyp, anyp, anyp, anyp, anyp, anyp, vmem),
        scratch_shapes=[
            pltpu.VMEM((total, NZ, rows, cw), BF16),
            pltpu.VMEM((total, PLANE, ROWS, cw), BF16),
            pltpu.VMEM((total, 2, ROWS, cw), BF16),
            pltpu.VMEM((NZ, 2, PLANE, rows), F32),
            pltpu.VMEM((NZ, 2, PLANE, rows), F32),
            pltpu.VMEM((PLANE * ROWS, NZ * rows), BF16),
            pltpu.VMEM((PLANE, ROWS, rows), BF16),
            pltpu.VMEM((2, ROWS, rows), BF16),
            dma((total,)),
            dma((NZ,)),
            dma((NZ,)),
            dma((total, 2, 4)),
            dma((total, 2, 4)),
            dma((total + 1,)),
            dma((total + 1,)),
            dma((total + 1, 2)),
            dma((total + 1,)),
            dma((3, 2, 2)),
            dma((3, 2, 2)),
            dma((3,)),
        ],
        compiler_params=pltpu.CompilerParams(
            collective_id=0, has_side_effects=True, vmem_limit_bytes=60 * 1024 * 1024
        ),
        name="dispatch",
    )(tokens, cotangent, routes, probs, slots, gate, up, down)


def combine_kernel(
    width,
    chunks,
    dx,
    dp,
    key,
    routes,
    slots,
    part_gate,
    part_up,
    part_down,
    out_tok,
    out_prob,
    out_gate,
    out_up,
    out_down,
    rbuf,
    relay,
    spread,
    gbuf,
    zout,
    zin,
    pbuf,
    prelay,
    maps_own,
    maps,
    wbuf0,
    wbuf1,
    wbuf2,
    wout0,
    wout1,
    wout2,
    win0,
    win1,
    win2,
    map_send,
    map_recv,
    z_send,
    z_recv,
    y_send,
    y_recv,
    r_recv,
    y_own,
    w_send,
    w_recv,
    w_own,
):
    me = Place()
    cw = width // chunks
    half = cw // 2
    rows = out_tok.shape[0]
    last = chunks
    parts = ((part_gate, wbuf0, wout0, win0, out_gate), (part_up, wbuf1, wout1, win1, out_up))
    parts = parts + ((part_down, wbuf2, wout2, win2, out_down),)
    way = (1, -1, 1)

    def w_block(n, owner):
        src = parts[n][0]
        if n < 2:
            return src.at[pl.ds(pl.multiple_of(owner * out_gate.shape[0], 128), out_gate.shape[0])]
        return src.at[:, pl.ds(pl.multiple_of(owner * out_down.shape[1], 128), out_down.shape[1])]

    def w_load(n, b):
        return pltpu.make_async_copy(w_block(n, mod(me.x + b, NX)), parts[n][1].at[b], w_own.at[n, b])

    for n in range(3):
        for b in range(NX):
            w_load(n, b).start()

    lane = lax.broadcasted_iota(jnp.int32, (NZ * rows, 128), 1).astype(F32)
    turned = key[...].T
    for j in range(PLANE * ROWS // 128):
        tile = jnp.zeros((NZ * rows, 128), F32)
        for d in range(128 * j // ROWS, (128 * j + 127) // ROWS + 1):
            mine = turned[:, d : d + 1]
            where = jnp.where(mine >= 0.0, mine + float(d * ROWS - 128 * j), -1.0)
            tile = tile + jnp.where(where == lane, 1.0, 0.0)
        spread[:, j * 128 : (j + 1) * 128] = tile.astype(BF16)

    greet(me)

    def cols(k):
        return pl.ds(pl.multiple_of(k * cw, cw), cw)

    def piece(k):
        return lambda d: dx.at[d, :, cols(k)]

    def landing(k):
        return lambda slot: rbuf.at[k, slot]

    def relay_of(k):
        return lambda core: relay.at[k, core]

    def relay_sem(k):
        return lambda core: r_recv.at[k, core]

    def y_start(k):
        plane_send(me, piece(k), landing(k), relay_of(k), y_send.at[k], y_recv.at[k], relay_sem(k))
        pltpu.make_async_copy(piece(k)(me.plane), rbuf.at[k, me.plane], y_own.at[k]).start()

    def y_pass(k):
        plane_relay(me, landing(k), relay_of(k), y_send.at[k], y_recv.at[k], relay_sem(k))

    def p_land(slot):
        return pbuf.at[slot]

    def p_relay(core):
        return prelay.at[core]

    def p_sem(core):
        return r_recv.at[last, core]

    plane_send(me, lambda d: dp.at[d], p_land, p_relay, y_send.at[last], y_recv.at[last], p_sem)
    pltpu.make_async_copy(dp.at[me.plane], pbuf.at[me.plane], y_own.at[last]).start()
    y_start(0)
    plane_relay(me, p_land, p_relay, y_send.at[last], y_recv.at[last], p_sem)

    def w_copy(n, hop):
        sign = way[n] if hop < 2 else -way[n]
        return remote(
            parts[n][2].at[hop], parts[n][3].at[hop], w_send.at[n, hop], w_recv.at[n, hop], me.at_x(sign)
        )

    def w_first():
        for n in range(3):
            for b in range(NX):
                w_load(n, b).wait()
            parts[n][2][0] = parts[n][1][2].astype(BF16)
            parts[n][2][2] = parts[n][1][(NX - way[n]) % NX].astype(BF16)
        for n in range(3):
            w_copy(n, 0).start()
            w_copy(n, 2).start()

    def w_second():
        for n in range(3):
            w_copy(n, 0).wait_recv()
            summed = parts[n][1][way[n] % NX] + parts[n][3][0].astype(F32)
            parts[n][2][1] = summed.astype(BF16)
        for n in range(3):
            w_copy(n, 1).start()

    def w_third():
        for n in range(3):
            w_copy(n, 1).wait_recv()
            w_copy(n, 2).wait_recv()
            parts[n][4][...] = parts[n][1][0] + parts[n][3][1].astype(F32) + parts[n][3][2].astype(F32)

    w_first()

    def z_copy(k, direction, stage):
        sign = 1 - 2 * direction
        if stage == 0:
            part = pl.ds(direction * half, half)
            src, dst = zout.at[k, direction, 0, :, part], zin.at[k, direction, 0, :, part]
        else:
            src, dst = zout.at[k, direction, stage], zin.at[k, direction, stage]
        return remote(src, dst, z_send.at[k, direction, stage], z_recv.at[k, direction, stage], me.at_z(sign))

    def z_stage(k, stage):
        for direction in (0, 1):
            sign = 1 - 2 * direction
            block = mod(me.z + sign * (4 - stage), NZ)
            if stage == 0:
                part = slice(direction * half, (direction + 1) * half)
                zout[k, direction, 0, :, part] = gbuf[k, block, :, part].astype(BF16)
            else:
                z_copy(k, direction, stage - 1).wait_recv()
                if stage == 1:
                    near = slice(direction * half, (direction + 1) * half)
                    rest = slice((1 - direction) * half, (2 - direction) * half)
                    summed = gbuf[k, block, :, near] + zin[k, direction, 0, :, near].astype(F32)
                    zout[k, direction, 1, :, near] = summed.astype(BF16)
                    zout[k, direction, 1, :, rest] = gbuf[k, block, :, rest].astype(BF16)
                else:
                    summed = gbuf[k, block] + zin[k, direction, stage - 1].astype(F32)
                    zout[k, direction, stage] = summed.astype(BF16)
            z_copy(k, direction, stage).start()

    def z_finish(k):
        z_copy(k, 0, 3).wait_recv()
        z_copy(k, 1, 3).wait_recv()
        summed = gbuf[k, me.z] + zin[k, 0, 3].astype(F32) + zin[k, 1, 3].astype(F32)
        out_tok[:, cols(k)] = summed.astype(BF16)

    def y_wait(k):
        seven = rbuf.at[k, pl.ds(0, PLANE - 1)]
        remote(seven, seven, y_send.at[k], y_recv.at[k], me.at_y(1, 0)).wait_recv()
        pltpu.make_async_copy(piece(k)(me.plane), rbuf.at[k, me.plane], y_own.at[k]).wait()

    def map_copy(s):
        z = mod(me.z + s, NZ)
        return remote(maps_own.at[z], maps.at[me.z], map_send.at[s], map_recv.at[s], me.at_z(s))

    def prob_grads():
        seven = pbuf.at[pl.ds(0, PLANE - 1)]
        remote(seven, seven, y_send.at[last], y_recv.at[last], me.at_y(1, 0)).wait_recv()
        pltpu.make_async_copy(dp.at[me.plane], pbuf.at[me.plane], y_own.at[last]).wait()
        row = lax.broadcasted_iota(jnp.int32, (ROWS, rows), 0).astype(F32)
        for d in range(PLANE):
            given = pbuf[d].astype(F32)
            for z in range(NZ):
                taken = key[d : d + 1, z * rows : (z + 1) * rows] == row
                maps_own[z, d : d + 1, :] = jnp.sum(jnp.where(taken, given, 0.0), axis=0, keepdims=True)
        maps[me.z] = maps_own[me.z]
        for s in range(1, NZ):
            map_copy(s).start()

    def step(i, carry):
        @pl.when((i >= 1) & (i < chunks))
        def _():
            y_start(i)

        @pl.when((i >= 1) & (i <= chunks))
        def _():
            y_pass(i - 1)

        @pl.when((i >= 3) & (i <= chunks + 2))
        def _():
            z_stage(i - 3, 2)

        @pl.when((i >= 2) & (i <= chunks + 1))
        def _():
            k = i - 2
            y_wait(k)
            got = rbuf[k].reshape(PLANE * ROWS, cw)
            gbuf[k] = jnp.dot(spread[...], got, preferred_element_type=F32).reshape(NZ, rows, cw)
            z_stage(k, 0)

        @pl.when((i >= 3) & (i <= chunks + 2))
        def _():
            z_stage(i - 3, 3)

        @pl.when(i == 2)
        def _():
            prob_grads()

        @pl.when((i >= 2) & (i <= chunks + 1))
        def _():
            z_stage(i - 2, 1)

        @pl.when((i >= 3) & (i <= chunks + 2))
        def _():
            z_finish(i - 3)

        @pl.when(i == 3)
        def _():
            w_second()

        return carry

    lax.fori_loop(0, chunks + 3, step, 0)
    w_third()
    for s in range(1, NZ):
        z = mod(me.z - s, NZ)
        remote(maps.at[z], maps.at[z], map_send.at[s], map_recv.at[s], me.at_z(s)).wait_recv()
    named = slots[...]
    given = maps[...].reshape(NZ * PLANE, rows)
    for k in range(routes.shape[0]):
        same = named == routes[k : k + 1, :]
        out_prob[k : k + 1, :] = jnp.sum(jnp.where(same, given, 0.0), axis=0, keepdims=True)

    def drain(k, carry):
        for direction in (0, 1):
            for stage in range(4):
                z_copy(k, direction, stage).wait_send()
        seven, two = rbuf.at[k, pl.ds(0, PLANE - 1)], rbuf.at[k, pl.ds(0, 2)]
        remote(seven, seven, y_send.at[k], y_recv.at[k], me.at_y(1, 0)).wait_send()
        remote(two, two, y_send.at[k], y_recv.at[k], me.at_y(1, 0)).wait_send()
        return carry

    lax.fori_loop(0, chunks, drain, 0)
    seven, two = pbuf.at[pl.ds(0, PLANE - 1)], pbuf.at[pl.ds(0, 2)]
    remote(seven, seven, y_send.at[last], y_recv.at[last], me.at_y(1, 0)).wait_send()
    remote(two, two, y_send.at[last], y_recv.at[last], me.at_y(1, 0)).wait_send()
    for s in range(1, NZ):
        map_copy(s).wait_send()
    for n in range(3):
        for hop in range(3):
            w_copy(n, hop).wait_send()


def combine(dx, dp, key, routes, slots, part_gate, part_up, part_down, chunks=4):
    _, _, width = dx.shape
    rows = dp.shape[2]
    cw = width // chunks
    depth, ff = part_gate.shape[0] // NX, part_gate.shape[1]
    dma = pltpu.SemaphoreType.DMA
    vmem = pl.BlockSpec(memory_space=pltpu.VMEM)
    anyp = pl.BlockSpec(memory_space=pl.ANY)
    shape = jax.ShapeDtypeStruct
    one, two = (depth, ff), (ff, width // NX)
    return pl.pallas_call(
        functools.partial(combine_kernel, width, chunks),
        out_shape=(
            shape((rows, width), BF16),
            shape(routes.shape, F32),
            shape(one, F32),
            shape(one, F32),
            shape(two, F32),
        ),
        in_specs=[anyp, anyp, vmem, vmem, vmem, anyp, anyp, anyp],
        out_specs=(vmem, vmem, vmem, vmem, vmem),
        scratch_shapes=[
            pltpu.VMEM((chunks, PLANE, ROWS, cw), BF16),
            pltpu.VMEM((chunks, 2, ROWS, cw), BF16),
            pltpu.VMEM((NZ * rows, PLANE * ROWS), BF16),
            pltpu.VMEM((chunks, NZ, rows, cw), F32),
            pltpu.VMEM((chunks, 2, 4, rows, cw), BF16),
            pltpu.VMEM((chunks, 2, 4, rows, cw), BF16),
            pltpu.VMEM((PLANE, ROWS, rows), BF16),
            pltpu.VMEM((2, ROWS, rows), BF16),
            pltpu.VMEM((NZ, PLANE, rows), F32),
            pltpu.VMEM((NZ, PLANE, rows), F32),
            pltpu.VMEM((NX,) + one, F32),
            pltpu.VMEM((NX,) + one, F32),
            pltpu.VMEM((NX,) + two, F32),
            pltpu.VMEM((3,) + one, BF16),
            pltpu.VMEM((3,) + one, BF16),
            pltpu.VMEM((3,) + two, BF16),
            pltpu.VMEM((3,) + one, BF16),
            pltpu.VMEM((3,) + one, BF16),
            pltpu.VMEM((3,) + two, BF16),
            dma((NZ,)),
            dma((NZ,)),
            dma((chunks, 2, 4)),
            dma((chunks, 2, 4)),
            dma((chunks + 1,)),
            dma((chunks + 1,)),
            dma((chunks + 1, 2)),
            dma((chunks + 1,)),
            dma((3, 3)),
            dma((3, 3)),
            dma((3, NX)),
        ],
        compiler_params=pltpu.CompilerParams(
            collective_id=1, has_side_effects=True, vmem_limit_bytes=62 * 1024 * 1024
        ),
        name="combine",
    )(dx, dp, key, routes, slots, part_gate, part_up, part_down)


def shards(tokens, cotangent, routes, probs, slot_expert, gate_w, up_w, down_w):
    rows, width = tokens.shape
    ff = gate_w.shape[2]
    by_plane = slot_expert.reshape(NY, NZ, NC).transpose(1, 0, 2).reshape(-1)
    slots = jnp.broadcast_to(by_plane[:, None], (by_plane.shape[0], rows))
    turned = routes.T
    x, dy, p, w_gate, w_up, w_down, key = dispatch(
        tokens, cotangent, turned, probs.T.astype(F32), slots, gate_w[0], up_w[0], down_w[0]
    )
    total = PLANE * ROWS
    x, dy = x.reshape(total, width), dy.reshape(total, width)
    weight = p.reshape(total, rows)[:, :1].astype(F32)
    w_gate, w_up = w_gate.reshape(width, ff), w_up.reshape(width, ff)
    gate = jnp.dot(x, w_gate, preferred_element_type=F32)
    upval = jnp.dot(x, w_up, preferred_element_type=F32)
    sig = jax.nn.sigmoid(gate)
    act = gate * sig
    hidden = (act * upval).astype(BF16)
    back = lax.dot_general(dy, w_down, (((1,), (1,)), ((), ())), preferred_element_type=F32)
    dprob = jnp.sum(hidden.astype(F32) * back, axis=1, keepdims=True).astype(BF16)
    dh = weight * back
    d_gate = (dh * upval * sig * (1.0 + gate * (1.0 - sig))).astype(BF16)
    d_up = (dh * act).astype(BF16)
    wide = (((1,), (1,)), ((), ()))
    dx = (
        lax.dot_general(d_gate, w_gate, wide, preferred_element_type=F32)
        + lax.dot_general(d_up, w_up, wide, preferred_element_type=F32)
    ).astype(BF16)
    wdy = (weight * dy.astype(F32)).astype(BF16)
    tall = (((0,), (0,)), ((), ()))
    part_gate = lax.dot_general(x, d_gate, tall, preferred_element_type=F32)
    part_up = lax.dot_general(x, d_up, tall, preferred_element_type=F32)
    part_down = lax.dot_general(hidden, wdy, tall, preferred_element_type=F32)
    grad_tokens, grad_probs, grad_gate, grad_up, grad_down = combine(
        dx.reshape(PLANE, ROWS, width),
        jnp.broadcast_to(dprob, (total, rows)).reshape(PLANE, ROWS, rows),
        key,
        turned,
        slots,
        part_gate,
        part_up,
        part_down,
    )
    return (
        grad_tokens,
        grad_probs.T.astype(BF16),
        grad_gate[None],
        grad_up[None],
        grad_down[None],
    )


def solution(mesh):
    placed = (
        P(("dp", "expert"), None),
        P(("dp", "expert"), None),
        P(("dp", "expert"), None),
        P(("dp", "expert"), None),
        P(),
        P("expert", "dp", None),
        P("expert", "dp", None),
        P("expert", None, "dp"),
    )
    return jax.shard_map(
        shards,
        mesh=mesh,
        in_specs=placed,
        out_specs=(
            P(("dp", "expert"), None),
            P(("dp", "expert"), None),
            P("expert", "dp", None),
            P("expert", "dp", None),
            P("expert", None, "dp"),
        ),
        check_vma=False,
    )
```

time: 593 us -> 296 us (0.50); the launches traced: 583 us -> 296 us
  waiting for transfers between devices: 388 us -> 0 us
  Pallas kernels: 0 us -> 242 us
  starting transfers between devices: 35.4 us -> 0 us
  other arithmetic: 31.9 us -> 2.64 us
  matrix products: 67 us -> 41.4 us
  local copies, waits for them, and re-layouts: 31.9 us -> 8.56 us
  between operations: 14.5 us -> 0.75 us
  blocking collectives: 13.5 us -> 0 us
    all_to_all x4 -> x0, waiting for transfers between devices: 310 us -> none  [the longest x1 129 us: shards(): lax.all_to_all(dx_rows.reshape(n_exp, local * CAP, width), 'expert', spli...]
    pallas_call x0 -> x2, Pallas kernels: none -> 242 us  [the longest x1 149 us: dispatch(): pl.pallas_call(functools.partial(dispatch_kernel, width, chunks), out_sha...]
    all_gather x3 -> x0, waiting for transfers between devices: 76.7 us -> none  [the longest x1 30.6 us: shards(): lax.all_gather(gate_w, 'dp', axis=1, tiled=True)]
    all_to_all x4 -> x0, starting transfers between devices: 34.4 us -> none  [the longest x1 12.1 us: shards(): lax.all_to_all(send_x, 'expert', split_axis=0, concat_axis=0, tiled=True)]
    dot_general x11 -> x8, matrix products: 67 us -> 41.4 us  [the longest x1 7.15 us: shards(): part_up = lax.dot_general(x, d_up, tall, preferred_element_type=F32)]
    reshape x4 -> x1, local copies, waits for them, and re-layouts: 23 us -> 0.75 us  [shards(): by_plane = slot_expert.reshape(NY, NZ, NC).transpose(1, 0, 2).reshape(-1)]
    another operation x4 -> x0, other arithmetic: 21.6 us -> none
    all_to_all x1 -> x0, blocking collectives: 13.5 us -> none  [shards(): lax.all_to_all(send_p, 'expert', split_axis=0, concat_axis=0, tiled=True)]
  transfers between devices with their start and end apart: 10 -> 0, of which waited for: 7 -> 0; matrix products, arithmetic and copies ran while one was open for 12% -> 0% of each run, Pallas kernels for 0% -> 0%
where the time goes in v1:
time: 296 us
  Pallas kernels  242 us (82%)
  matrix products  41.4 us (14%)
  local copies, waits for them, and re-layouts  8.56 us (3%)
    pallas_call x1, Pallas kernels, dispatch(): pl.pallas_call(functools.partial(dispatch_kernel, width, chunks), out_sha...  149 us
    pallas_call x1, Pallas kernels, combine(): pl.pallas_call(functools.partial(combine_kernel, width, chunks), out_shap...  93.5 us
    dot_general x1, matrix products, shards(): part_up = lax.dot_general(x, d_up, tall, preferred_element_type=F32)  7.15 us
    dot_general x1, matrix products, shards(): gate = jnp.dot(x, w_gate, preferred_element_type=F32)  6.44 us
    dot_general x1, matrix products, shards(): part_down = lax.dot_general(hidden, wdy, tall, preferred_element_type=F32)  6.38 us
    dot_general x1, matrix products, shards(): lax.dot_general(dy, w_down, (((1,), (1,)), ((), ())), preferred_element_t...  6.22 us
    unnamed x23, local copies, waits for them, and re-layouts  5.97 us

profile of v1, /device:TPU:32, one launch (start us, length us, event | category | flops | bytes accessed | tf_op | source)
XLA Modules:
  0.0 295.6 jit_solution(13381765205515572530)
XLA Ops:
  0.6 0.7 reshape.44
  1.4 0.1 broadcast_in_dim.22
  1.5 0.7 broadcast_in_dim.23.slots
  2.2 1.3 convert_bitcast_fusion.probs
  3.5 148.7 %dispatch.1 = (bf16[8,144,2048]{2,1,0:T(8,128)(2,1)}, bf16[8,144,2048]{2,1,0:T(8,128)(2,1)}, bf16[8,144,128]{2,1,0:T(8,128)(2,1)}, bf16[4,512,384]{2,1,0:T(8,128...) custom-call(bf16[128,2048]{1,0:T(8,128)(2,1)} %tok.1, bf16[128,2048]{1,0:T(8,128)(2,1)} %cot.1, ...), custom_call_target="tpu_custom_call" | custom-call | tf_op jit(solution)/shard_map/dispatch/pallas_call | solution.py:383
  152.2 0.0 copy-start.1
  152.2 0.0 copy-start.5
  152.2 6.4 %fusion.5 = f32[1152,384]{0,1:T(8,128)} fusion(bf16[1152,2048]{1,0:T(8,128)(2,1)} %bitcast.49, bf16[2048,384]{1,0:T(8,128)(2,1)} %bitcast.35), kind=kOutput, calls=%fused_computation.15 | convolution fusion | flops 1811939328 | bytes 8060928 | tf_op jit(solution)/shard_map/dot_general | solution.py:779
  158.6 0.0 copy-done.1
  158.6 0.0 copy-done.5
  158.6 0.0 copy-start.4
  158.6 0.0 copy-start.6
  158.6 3.7 %fusion.4 = f32[1152,384]{0,1:T(8,128)} fusion(bf16[1152,2048]{1,0:T(8,128)(2,1)S(1)} %bitcast.51, bf16[2048,384]{1,0:T(8,128)(2,1)S(1)} %bitcast.37), kind=kOutput, calls=%fused_computation.14 | convolution fusion | flops 1811939328 | bytes 8060928 | tf_op jit(solution)/shard_map/dot_general | solution.py:780
  162.3 0.0 copy-done.4
  162.3 0.2 copy.16
  162.5 0.0 copy-done.6
  162.5 6.2 %multiply_reduce_fusion = (bf16[1152]{0:T(1024)(128)(2,1)S(1)}, bf16[1152,384]{0,1:T(8,128)(2,1)S(1)}, bf16[1152,384]{0,1:T(8,128)(2,1)S(1)}, bf16[1152,384]{0,1:T(8,128)(2,1)S(1)}) fusion(f32[1152,384]{0,1:T(8,128)} %fusion.4, f32[1152,384]{0,1:T(8,128)} %fusion.5, f32[1152]{0:T(1024)S(1)} %convert_reduce_fusion, bf16[1152,2048]{1,0:T(8,128)(2,1)} %bitcast.55, ...), kind=kOutput, calls=%fused_computation.5 | convolution fusion | flops 1820343168 | bytes 12491520 | tf_op jit(solution)/shard_map/dot_general | solution.py:784
  168.7 0.0 slice-start
  168.7 6.4 %fusion.1.part_down = f32[384,2048]{1,0:T(8,128)} fusion(bf16[1152,384]{0,1:T(8,128)(2,1)S(1)} %get-tuple-element.30, bf16[1152,2048]{1,0:T(8,128)(2,1)} %bitcast.56, f32[1152]{0:T(1024)S(1)} %convert_reduce_fusion), kind=kOutput, calls=%fused_computation.3 | convolution fusion | flops 1819017216 | bytes 8753664 | tf_op jit(solution)/shard_map/dot_general | solution.py:798
  175.1 0.0 slice-start.1
  175.1 7.2 %fusion.8.part_up = f32[2048,384]{1,0:T(8,128)} fusion(bf16[1152,2048]{1,0:T(8,128)(2,1)} %bitcast.50, bf16[1152,384]{0,1:T(8,128)(2,1)S(1)} %get-tuple-element.32), kind=kOutput, calls=%fused_computation.18 | convolution fusion | flops 1811939328 | bytes 8749056 | tf_op jit(solution)/shard_map/dot_general | solution.py:797
  182.3 0.0 slice-done
  182.3 0.0 slice-done.1
  182.3 0.0 copy-start
  182.3 4.5 %fusion.7.part_gate = f32[2048,384]{1,0:T(8,128)} fusion(bf16[1152,2048]{1,0:T(8,128)(2,1)S(1)} %bitcast.54, bf16[1152,384]{0,1:T(8,128)(2,1)S(1)} %get-tuple-element.31), kind=kOutput, calls=%fused_computation.17 | convolution fusion | flops 1811939328 | bytes 8749056 | tf_op jit(solution)/shard_map/dot_general | solution.py:796
  186.8 0.0 copy-done
  186.8 2.7 fusion.6
  189.5 4.4 %fusion = bf16[1152,2048]{1,0:T(8,128)(2,1)} fusion(f32[1152,2048]{1,0:T(8,128)S(1)} %fusion.6, bf16[1152,384]{0,1:T(8,128)(2,1)S(1)} %get-tuple-element.32, bf16[2048,384]{1,0:T(8,128)(2,1)S(1)} %bitcast.38), kind=kOutput, calls=%fused_computation.2 | convolution fusion | flops 1816657920 | bytes 16613376 | tf_op jit(solution)/shard_map/dot_general | solution.py:792
  193.8 0.1 convert_element_type.52
  193.9 0.9 broadcast_in_dim.24.dp
  194.9 93.5 %combine.1 = (bf16[128,2048]{1,0:T(8,128)(2,1)}, f32[8,128]{1,0:T(8,128)}, f32[512,384]{1,0:T(8,128)}, f32[512,384]{1,0:T(8,128)}, f32[384,512]{1,0:T(8,128)}) custom-call(bf16[8,144,2048]{2,1,0:T(8,128)(2,1)} %bitcast.34, bf16[8,144,128]{2,1,0:T(8,128)(2,1)} %broadcast_in_dim.24.dp, f32[8,1024]{1,0:T(8,128)} %get-tuple-element.23.key, s32[8,128]{1,0:T(8,128)} %bitcast.48, ...), custom_call_target="tpu_custom_call" | custom-call | tf_op jit(solution)/shard_map/combine/pallas_call | solution.py:716
  288.4 0.0 copy-start.3
  288.4 1.3 convert_bitcast_fusion.1
  289.8 1.9 copy.21
  291.7 0.0 copy-start.2
  291.7 2.1 copy.22
  293.8 0.0 copy-done.3
  293.8 0.9 copy.23
  294.7 0.0 copy-done.2
  294.7 0.9 copy.24
  (3 shorter events, 0.0 us)
Async XLA Ops:
  152.2 6.5 %copy-start.1 = (bf16[4,512,384]{2,1,0:T(8,128)(2,1)S(1)}, bf16[4,512,384]{2,1,0:T(8,128)(2,1)}, u32[]{:S(2)}) copy-start(bf16[4,512,384]{2,1,0:T(8,128)(2,1)} %get-tuple-element.21) | copy-start | bytes 4718596
  152.2 6.5 %copy-start.5 = (bf16[8,144,2048]{2,1,0:T(8,128)(2,1)S(1)}, bf16[8,144,2048]{2,1,0:T(8,128)(2,1)}, u32[]{:S(2)}) copy-start(bf16[8,144,2048]{2,1,0:T(8,128)(2,1)} %get-tuple-element.20) | copy-start | bytes 14155780
  158.6 3.7 %copy-start.4 = (bf16[8,144,128]{2,1,0:T(8,128)(2,1)S(1)}, bf16[8,144,128]{2,1,0:T(8,128)(2,1)}, u32[]{:S(2)}) copy-start(bf16[8,144,128]{2,1,0:T(8,128)(2,1)} %get-tuple-element.17) | copy-start | bytes 884740
  158.6 3.9 %copy-start.6 = (bf16[384,2048]{1,0:T(8,128)(2,1)S(1)}, bf16[384,2048]{1,0:T(8,128)(2,1)}, u32[]{:S(2)}) copy-start(bf16[384,2048]{1,0:T(8,128)(2,1)} %get-tuple-element.19) | copy-start | bytes 4718596
  168.7 13.5 %slice-start = ((s8[4718592]{0:T(1024)(128)(4,1)}), s8[524288]{0:T(1024)(128)(4,1)S(1)}, s32[]{:S(2)}) async-start(s8[4718592]{0:T(1024)(128)(4,1)} %bitcast.52), calls=%async_computation | async-start | bytes 1048576
  175.1 7.2 %slice-start.1 = ((s8[4718592]{0:T(1024)(128)(4,1)}), s8[4194304]{0:T(1024)(128)(4,1)S(1)}, s32[]{:S(2)}) async-start(s8[4718592]{0:T(1024)(128)(4,1)} %bitcast.52), calls=%async_computation.1 | async-start | bytes 8388608
  182.3 4.5 %copy-start = (bf16[4,512,384]{2,1,0:T(8,128)(2,1)S(1)}, bf16[4,512,384]{2,1,0:T(8,128)(2,1)}, u32[]{:S(2)}) copy-start(bf16[4,512,384]{2,1,0:T(8,128)(2,1)} %get-tuple-element.22) | copy-start | bytes 4718596
  288.4 5.4 %copy-start.3 = (f32[512,384]{1,0:T(8,128)S(1)}, f32[512,384]{1,0:T(8,128)}, u32[]{:S(2)}) copy-start(f32[512,384]{1,0:T(8,128)} %get-tuple-element.27) | copy-start | bytes 2359300
  291.7 3.0 %copy-start.2 = (f32[384,512]{1,0:T(8,128)S(1)}, f32[384,512]{1,0:T(8,128)}, u32[]{:S(2)}) copy-start(f32[384,512]{1,0:T(8,128)} %get-tuple-element.28) | copy-start | bytes 2359300

commit v2 on v1

--- a/solution.py
+++ b/solution.py
@@ -11,6 +11,7 @@
 NX, NY, NZ, NC = 4, 4, 8, 2
 PLANE = NY * NC
 ROWS = NZ * CAP
+LAG = 8
 MESH = pl.DeviceIdType.MESH
 F32 = jnp.float32
 BF16 = jnp.bfloat16
@@ -79,6 +80,14 @@
         remote(relay(core), relay(core), send, relay_recv(core), me.at_y(step, core)).wait_recv()
         origin = mod(me.y - step, NY) * NC + me.c
         remote(relay(core), landing(origin), send, recv, me.at_y(step, core)).start()
+
+
+def slot_rows(slot_expert, named):
+    for z in range(NZ):
+        for y in range(NY):
+            for c in range(NC):
+                at = z * PLANE + y * NC + c
+                named[at : at + 1, :] = jnp.full((1, named.shape[1]), slot_expert[(y * NZ + z) * NC + c], jnp.int32)
 
 
 def dispatch_kernel(
@@ -92,16 +101,23 @@
     gate,
     up,
     down,
-    out_x,
-    out_dy,
-    out_p,
-    all_gate,
-    all_up,
-    all_down,
+    out_rows,
+    out_wide,
+    out_grads,
+    out_dp,
     key_out,
     zbuf,
     sbuf,
     relay,
+    landed,
+    wide,
+    tall,
+    acc,
+    racc,
+    grads,
+    dp,
+    pin,
+    named,
     maps_own,
     maps,
     pick,
@@ -119,10 +135,13 @@
     w_send,
     w_recv,
     w_own,
+    out_sem,
 ):
     me = Place()
     cw = width // chunks
     half = cw // 2
+    ff = gate.shape[1]
+    depth = gate.shape[0]
     total = 2 * chunks
     rows = tok.shape[0]
 
@@ -137,11 +156,13 @@
 
     hit = jnp.zeros((NZ * PLANE, rows), F32)
     weight = jnp.zeros((NZ * PLANE, rows), F32)
-    named = slots[...]
-    for k in range(routes.shape[0]):
-        same = named == routes[k : k + 1, :]
+    slot_rows(slots, named)
+    turned = routes[...].T
+    shares = probs[...].astype(F32).T
+    for k in range(turned.shape[0]):
+        same = named[...] == turned[k : k + 1, :]
         hit = hit + jnp.where(same, 1.0, 0.0)
-        weight = weight + jnp.where(same, probs[k : k + 1, :], 0.0)
+        weight = weight + jnp.where(same, shares[k : k + 1, :], 0.0)
     before = lax.broadcasted_iota(jnp.int32, (rows, rows), 0) < lax.broadcasted_iota(
         jnp.int32, (rows, rows), 1
     )
@@ -187,18 +208,18 @@
             if stage < 4:
                 z_copy(k, direction, stage).start()
 
-    weights = ((gate, all_gate, True), (up, all_up, True), (down, all_down, False))
+    weights = (gate, up, down)
 
     def w_slot(n, owner):
-        src, dst, lead = weights[n]
-        if lead:
-            return dst.at[owner]
-        return dst.at[:, pl.ds(pl.multiple_of(owner * src.shape[1], 128), src.shape[1])]
+        if n < 2:
+            return wide.at[pl.ds(pl.multiple_of(owner * depth, 128), depth), pl.ds(n * ff, ff)]
+        part = down.shape[1]
+        return tall.at[:, pl.ds(pl.multiple_of(owner * part, 128), part)]
 
     def w_copy(n, direction, hop):
         sign = 1 - 2 * direction
         owner = me.x if hop == 0 else mod(me.x - sign, NX)
-        src = weights[n][0] if hop == 0 else w_slot(n, owner)
+        src = weights[n] if hop == 0 else w_slot(n, owner)
         return remote(
             src, w_slot(n, owner), w_send.at[n, direction, hop], w_recv.at[n, direction, hop], me.at_x(sign)
         )
@@ -217,7 +238,7 @@
     for n in range(3):
         for direction in (0, 1):
             w_copy(n, direction, 0).start()
-        pltpu.make_async_copy(weights[n][0], w_slot(n, me.x), w_own.at[n]).start()
+        pltpu.make_async_copy(weights[n], w_slot(n, me.x), w_own.at[n]).start()
 
     for s in range(1, NZ):
         z = mod(me.z - s, NZ)
@@ -244,40 +265,56 @@
     def relay_sem(k):
         return lambda core: r_recv.at[k, core]
 
-    def landing(k, out):
-        col = pl.multiple_of(lax.rem(k, chunks) * cw, cw)
-        return lambda slot: out.at[slot, :, pl.ds(col, cw)]
-
-    def by_array(k, act):
+    def landing(k):
+        return lambda slot: landed.at[k, slot]
+
+    def own_rows(k):
+        return pltpu.make_async_copy(sbuf.at[k, me.plane], landed.at[k, me.plane], y_own.at[k])
+
+    def send_chunk(k):
+        plane_send(me, piece(k), landing(k), relay_of(k), y_send.at[k], y_recv.at[k], relay_sem(k))
+        own_rows(k).start()
+
+    def relay_chunk(k):
+        plane_relay(me, landing(k), relay_of(k), y_send.at[k], y_recv.at[k], relay_sem(k))
+
+    def seven_of(k):
+        sent, here = sbuf.at[k, pl.ds(0, PLANE - 1)], landed.at[k, pl.ds(0, PLANE - 1)]
+        return remote(sent, here, y_send.at[k], y_recv.at[k], me.at_y(1, 0))
+
+    def rows_out(k):
+        return pltpu.make_async_copy(landed.at[k], out_rows.at[k], out_sem.at[k])
+
+    def consume(k):
+        seven_of(k).wait_recv()
+        own_rows(k).wait()
+
         @pl.when(k < chunks)
         def _():
-            act(out_x)
+            take = pl.ds(pl.multiple_of(k * cw, cw), cw)
+            acc[...] += jnp.dot(
+                landed[k].reshape(PLANE * ROWS, cw), wide[take, :], preferred_element_type=F32
+            )
 
         @pl.when(k >= chunks)
         def _():
-            act(out_dy)
-
-    def send_chunk(k):
-        def act(out):
-            plane_send(
-                me, piece(k), landing(k, out), relay_of(k), y_send.at[k], y_recv.at[k], relay_sem(k)
+            take = pl.ds(pl.multiple_of((k - chunks) * cw, cw), cw)
+            racc[...] += lax.dot_general(
+                landed[k].reshape(PLANE * ROWS, cw),
+                tall[:, take],
+                (((1,), (1,)), ((), ())),
+                preferred_element_type=F32,
             )
-            pltpu.make_async_copy(
-                sbuf.at[k, me.plane], landing(k, out)(me.plane), y_own.at[k]
-            ).start()
-
-        by_array(k, act)
-
-    def relay_chunk(k):
-        by_array(
-            k,
-            lambda out: plane_relay(
-                me, landing(k, out), relay_of(k), y_send.at[k], y_recv.at[k], relay_sem(k)
-            ),
-        )
+            for d in range(PLANE):
+                for j in range(cw // rows):
+                    part = slice(j * rows, (j + 1) * rows)
+                    scaled = landed[k, d, :, part].astype(F32) * pin[d].astype(F32)
+                    landed[k, d, :, part] = scaled.astype(BF16)
+
+        rows_out(k).start()
 
     def p_land(slot):
-        return out_p.at[slot]
+        return pin.at[slot]
 
     def p_relay(core):
         return prelay.at[core]
@@ -285,62 +322,103 @@
     def p_sem(core):
         return r_recv.at[last, core]
 
+    acc[...] = jnp.zeros_like(acc)
+    racc[...] = jnp.zeros_like(racc)
+
+    def wide_out(n):
+        if n == 0:
+            return pltpu.make_async_copy(wide, out_wide, out_sem.at[total])
+        return pltpu.make_async_copy(grads, out_grads, out_sem.at[total + 1])
+
+    def p_seven():
+        sent, here = pbuf.at[pl.ds(0, PLANE - 1)], pin.at[pl.ds(0, PLANE - 1)]
+        return remote(sent, here, y_send.at[last], y_recv.at[last], me.at_y(1, 0))
+
     def step(i, carry):
         @pl.when((i >= 1) & (i < total))
         def _():
             z_stage(i, 0)
 
-        @pl.when((i >= 1) & (i <= total))
-        def _():
-            z_stage(i - 1, 2)
-
-        @pl.when((i >= 2) & (i <= total + 1))
-        def _():
-            k = i - 2
+        for stage in (1, 2, 3):
+
+            @pl.when((i >= stage) & (i < total + stage))
+            def _(stage=stage):
+                z_stage(i - stage, stage)
+
+        @pl.when((i >= 4) & (i < total + 4))
+        def _():
+            k = i - 4
             z_stage(k, 4)
             block = zbuf[k].reshape(NZ * rows, cw)
             out = jnp.dot(pick[...], block, preferred_element_type=F32).astype(BF16)
             sbuf[k] = out.reshape(PLANE, ROWS, cw)
             send_chunk(k)
 
-        @pl.when(i < total)
-        def _():
-            z_stage(i, 1)
-
-        @pl.when((i >= 1) & (i <= total))
-        def _():
-            z_stage(i - 1, 3)
-
-        @pl.when((i >= 3) & (i <= total + 2))
-        def _():
-            relay_chunk(i - 3)
-
-        @pl.when(i == 1)
+        @pl.when((i >= 6) & (i < total + 6))
+        def _():
+            relay_chunk(i - 6)
+
+        @pl.when(i == 5)
         def _():
             for n in range(3):
                 for direction in (0, 1):
                     w_wait(n, direction, 0)
                 w_copy(n, 0 if n < 2 else 1, 1).start()
 
-        @pl.when(i == 2)
+        @pl.when(i == 6)
         def _():
             plane_send(me, lambda d: pbuf.at[d], p_land, p_relay, y_send.at[last], y_recv.at[last], p_sem)
-            pltpu.make_async_copy(pbuf.at[me.plane], out_p.at[me.plane], y_own.at[last]).start()
-
-        @pl.when(i == 3)
+            pltpu.make_async_copy(pbuf.at[me.plane], pin.at[me.plane], y_own.at[last]).start()
+
+        @pl.when(i == 8)
         def _():
             plane_relay(me, p_land, p_relay, y_send.at[last], y_recv.at[last], p_sem)
 
+        @pl.when(i == LAG)
+        def _():
+            for n in range(3):
+                w_wait(n, 0 if n < 2 else 1, 1)
+                pltpu.make_async_copy(weights[n], w_slot(n, me.x), w_own.at[n]).wait()
+            wide_out(0).start()
+
+        @pl.when(i == chunks + LAG)
+        def _():
+            p_seven().wait_recv()
+            pltpu.make_async_copy(pbuf.at[me.plane], pin.at[me.plane], y_own.at[last]).wait()
+
+        @pl.when((i >= LAG) & (i < total + LAG))
+        def _():
+            consume(i - LAG)
+
         return carry
 
-    lax.fori_loop(0, total + 3, step, 0)
+    lax.fori_loop(0, total + LAG, step, 0)
+
+    def point(d, carry):
+        these = pl.ds(pl.multiple_of(d * ROWS, 16), ROWS)
+        g, u, r = acc[these, :ff], acc[these, ff:], racc[these, :]
+        p = pin[d].astype(F32)
+        p = jnp.concatenate([p] * (ff // rows), axis=1)
+        sg = jax.nn.sigmoid(g)
+        act = g * sg
+        hidden = (act * u).astype(BF16)
+        given = jnp.sum(hidden.astype(F32) * r, axis=1, keepdims=True)
+        dp[d] = jnp.broadcast_to(given, (ROWS, rows)).astype(BF16)
+        dh = p * r
+        grads[these, :ff] = (dh * u * sg * (1.0 + g * (1.0 - sg))).astype(BF16)
+        grads[these, ff : 2 * ff] = (dh * act).astype(BF16)
+        grads[these, 2 * ff :] = hidden
+        return carry
+
+    lax.fori_loop(0, PLANE, point, 0)
+    dp_out = pltpu.make_async_copy(dp, out_dp, out_sem.at[total + 2])
+    wide_out(1).start()
+    dp_out.start()
 
     for n in range(3):
-        w_wait(n, 0 if n < 2 else 1, 1)
         for direction in (0, 1):
             w_copy(n, direction, 0).wait_send()
         w_copy(n, 0 if n < 2 else 1, 1).wait_send()
-        pltpu.make_async_copy(weights[n][0], w_slot(n, me.x), w_own.at[n]).wait()
     for s in range(1, NZ):
         z = mod(me.z + s, NZ)
         remote(maps_own.at[z], maps.at[me.z], map_send.at[s], map_recv.at[s], me.at_z(s)).wait_send()
@@ -349,30 +427,22 @@
         for direction in (0, 1):
             for stage in range(4):
                 z_copy(k, direction, stage).wait_send()
-
-        def act(out):
-            here = out.at[pl.ds(0, PLANE - 1), :, pl.ds(pl.multiple_of(lax.rem(k, chunks) * cw, cw), cw)]
-            sent = sbuf.at[k, pl.ds(0, PLANE - 1)]
-            remote(sent, here, y_send.at[k], y_recv.at[k], me.at_y(1, 0)).wait_recv()
-            remote(sent, here, y_send.at[k], y_recv.at[k], me.at_y(1, 0)).wait_send()
-            two = sbuf.at[k, pl.ds(0, 2)]
-            remote(two, two, y_send.at[k], y_recv.at[k], me.at_y(1, 0)).wait_send()
-            pltpu.make_async_copy(
-                sbuf.at[k, me.plane], landing(k, out)(me.plane), y_own.at[k]
-            ).wait()
-
-        by_array(k, act)
+        seven_of(k).wait_send()
+        two = sbuf.at[k, pl.ds(0, 2)]
+        remote(two, two, y_send.at[k], y_recv.at[k], me.at_y(1, 0)).wait_send()
+        rows_out(k).wait()
         return carry
 
     lax.fori_loop(0, total, drain, 0)
-    here, sent, two = out_p.at[pl.ds(0, PLANE - 1)], pbuf.at[pl.ds(0, PLANE - 1)], pbuf.at[pl.ds(0, 2)]
-    remote(sent, here, y_send.at[last], y_recv.at[last], me.at_y(1, 0)).wait_recv()
-    remote(sent, here, y_send.at[last], y_recv.at[last], me.at_y(1, 0)).wait_send()
+    two = pbuf.at[pl.ds(0, 2)]
+    p_seven().wait_send()
     remote(two, two, y_send.at[last], y_recv.at[last], me.at_y(1, 0)).wait_send()
-    pltpu.make_async_copy(pbuf.at[me.plane], out_p.at[me.plane], y_own.at[last]).wait()
-
-
-def dispatch(tokens, cotangent, routes, probs, slots, gate, up, down, chunks=4):
+    wide_out(0).wait()
+    wide_out(1).wait()
+    dp_out.wait()
+
+
+def dispatch(tokens, cotangent, routes, probs, slots, gate, up, down, chunks=8):
     rows, width = tokens.shape
     depth, ff = gate.shape
     cw, total = width // chunks, 2 * chunks
@@ -383,20 +453,27 @@
     return pl.pallas_call(
         functools.partial(dispatch_kernel, width, chunks),
         out_shape=(
-            shape((PLANE, ROWS, width), BF16),
-            shape((PLANE, ROWS, width), BF16),
+            shape((total, PLANE, ROWS, cw), BF16),
+            shape((NX * depth, 2 * ff), BF16),
+            shape((PLANE * ROWS, 3 * ff), BF16),
             shape((PLANE, ROWS, rows), BF16),
-            shape((NX, depth, ff), BF16),
-            shape((NX, depth, ff), BF16),
-            shape((ff, width), BF16),
             shape((PLANE, NZ * rows), F32),
         ),
-        in_specs=[anyp, anyp, vmem, vmem, vmem, vmem, vmem, vmem],
-        out_specs=(anyp, anyp, anyp, anyp, anyp, anyp, vmem),
+        in_specs=[anyp, anyp, vmem, vmem, pl.BlockSpec(memory_space=pltpu.SMEM), vmem, vmem, vmem],
+        out_specs=(anyp, anyp, anyp, anyp, vmem),
         scratch_shapes=[
             pltpu.VMEM((total, NZ, rows, cw), BF16),
             pltpu.VMEM((total, PLANE, ROWS, cw), BF16),
             pltpu.VMEM((total, 2, ROWS, cw), BF16),
+            pltpu.VMEM((total, PLANE, ROWS, cw), BF16),
+            pltpu.VMEM((NX * depth, 2 * ff), BF16),
+            pltpu.VMEM((ff, width), BF16),
+            pltpu.VMEM((PLANE * ROWS, 2 * ff), F32),
+            pltpu.VMEM((PLANE * ROWS, ff), F32),
+            pltpu.VMEM((PLANE * ROWS, 3 * ff), BF16),
+            pltpu.VMEM((PLANE, ROWS, rows), BF16),
+            pltpu.VMEM((PLANE, ROWS, rows), BF16),
+            pltpu.VMEM((NZ * PLANE, rows), jnp.int32),
             pltpu.VMEM((NZ, 2, PLANE, rows), F32),
             pltpu.VMEM((NZ, 2, PLANE, rows), F32),
             pltpu.VMEM((PLANE * ROWS, NZ * rows), BF16),
@@ -414,6 +491,7 @@
             dma((3, 2, 2)),
             dma((3, 2, 2)),
             dma((3,)),
+            dma((total + 3,)),
         ],
         compiler_params=pltpu.CompilerParams(
             collective_id=0, has_side_effects=True, vmem_limit_bytes=60 * 1024 * 1024
@@ -425,14 +503,13 @@
 def combine_kernel(
     width,
     chunks,
-    dx,
+    rows_in,
+    wide_in,
+    grads_in,
     dp,
     key,
     routes,
     slots,
-    part_gate,
-    part_up,
-    part_down,
     out_tok,
     out_prob,
     out_gate,
@@ -448,9 +525,14 @@
     prelay,
     maps_own,
     maps,
-    wbuf0,
-    wbuf1,
-    wbuf2,
+    kept,
+    wide,
+    grads,
+    dx,
+    named,
+    wmid0,
+    wmid1,
+    wmid2,
     wout0,
     wout1,
     wout2,
@@ -467,29 +549,31 @@
     y_own,
     w_send,
     w_recv,
-    w_own,
+    load_sem,
 ):
     me = Place()
     cw = width // chunks
     half = cw // 2
+    ff = out_gate.shape[1]
+    per = width // NX // cw
     rows = out_tok.shape[0]
     last = chunks
-    parts = ((part_gate, wbuf0, wout0, win0, out_gate), (part_up, wbuf1, wout1, win1, out_up))
-    parts = parts + ((part_down, wbuf2, wout2, win2, out_down),)
+    parts = ((wmid0, wout0, win0, out_gate), (wmid1, wout1, win1, out_up), (wmid2, wout2, win2, out_down))
     way = (1, -1, 1)
 
-    def w_block(n, owner):
-        src = parts[n][0]
-        if n < 2:
-            return src.at[pl.ds(pl.multiple_of(owner * out_gate.shape[0], 128), out_gate.shape[0])]
-        return src.at[:, pl.ds(pl.multiple_of(owner * out_down.shape[1], 128), out_down.shape[1])]
-
-    def w_load(n, b):
-        return pltpu.make_async_copy(w_block(n, mod(me.x + b, NX)), parts[n][1].at[b], w_own.at[n, b])
-
-    for n in range(3):
-        for b in range(NX):
-            w_load(n, b).start()
+    def load(n):
+        if n < chunks:
+            take = pl.ds(n * cw, cw)
+            return pltpu.make_async_copy(wide_in.at[take], wide.at[take], load_sem.at[n])
+        if n == chunks:
+            return pltpu.make_async_copy(grads_in, grads, load_sem.at[n])
+        return pltpu.make_async_copy(rows_in, kept, load_sem.at[n])
+
+    load(chunks).start()
+    for n in range(chunks):
+        load(n).start()
+    load(chunks + 1).start()
+    slot_rows(slots, named)
 
     lane = lax.broadcasted_iota(jnp.int32, (NZ * rows, 128), 1).astype(F32)
     turned = key[...].T
@@ -507,7 +591,7 @@
         return pl.ds(pl.multiple_of(k * cw, cw), cw)
 
     def piece(k):
-        return lambda d: dx.at[d, :, cols(k)]
+        return lambda d: dx.at[k, d]
 
     def landing(k):
         return lambda slot: rbuf.at[k, slot]
@@ -519,6 +603,10 @@
         return lambda core: r_recv.at[k, core]
 
     def y_start(k):
+        out = lax.dot_general(
+            grads[:, : 2 * ff], wide[cols(k), :], (((1,), (1,)), ((), ())), preferred_element_type=F32
+        )
+        dx[k] = out.astype(BF16).reshape(PLANE, ROWS, cw)
         plane_send(me, piece(k), landing(k), relay_of(k), y_send.at[k], y_recv.at[k], relay_sem(k))
         pltpu.make_async_copy(piece(k)(me.plane), rbuf.at[k, me.plane], y_own.at[k]).start()
 
@@ -536,30 +624,46 @@
 
     plane_send(me, lambda d: dp.at[d], p_land, p_relay, y_send.at[last], y_recv.at[last], p_sem)
     pltpu.make_async_copy(dp.at[me.plane], pbuf.at[me.plane], y_own.at[last]).start()
+    load(chunks).wait()
+    for n in range(chunks):
+        load(n).wait()
     y_start(0)
+    y_start(1)
     plane_relay(me, p_land, p_relay, y_send.at[last], y_recv.at[last], p_sem)
 
     def w_copy(n, hop):
         sign = way[n] if hop < 2 else -way[n]
         return remote(
-            parts[n][2].at[hop], parts[n][3].at[hop], w_send.at[n, hop], w_recv.at[n, hop], me.at_x(sign)
+            parts[n][1].at[hop], parts[n][2].at[hop], w_send.at[n, hop], w_recv.at[n, hop], me.at_x(sign)
         )
 
-    def w_first():
-        for n in range(3):
-            for b in range(NX):
-                w_load(n, b).wait()
-            parts[n][2][0] = parts[n][1][2].astype(BF16)
-            parts[n][2][2] = parts[n][1][(NX - way[n]) % NX].astype(BF16)
-        for n in range(3):
-            w_copy(n, 0).start()
-            w_copy(n, 2).start()
+    def put(n, off, j, value):
+        where = (slice(j * cw, (j + 1) * cw), slice(None))
+        if n == 2:
+            where = where[::-1]
+        if off == 0:
+            parts[n][3][where] = value
+        elif off == way[n]:
+            parts[n][0][where] = value
+        else:
+            parts[n][1][(0 if off == 2 else 2,) + where] = value.astype(BF16)
+
+    def w_block(off):
+        owner = mod(me.x + off, NX)
+        down_to = (((0,), (0,)), ((), ()))
+        for j in range(per):
+            x = kept[owner * per + j].reshape(PLANE * ROWS, cw)
+            w = kept[chunks + owner * per + j].reshape(PLANE * ROWS, cw)
+            both = lax.dot_general(x, grads[:, : 2 * ff], down_to, preferred_element_type=F32)
+            put(0, off, j, both[:, :ff])
+            put(1, off, j, both[:, ff:])
+            put(2, off, j, lax.dot_general(grads[:, 2 * ff :], w, down_to, preferred_element_type=F32))
 
     def w_second():
         for n in range(3):
             w_copy(n, 0).wait_recv()
-            summed = parts[n][1][way[n] % NX] + parts[n][3][0].astype(F32)
-            parts[n][2][1] = summed.astype(BF16)
+            summed = parts[n][0][...] + parts[n][2][0].astype(F32)
+            parts[n][1][1] = summed.astype(BF16)
         for n in range(3):
             w_copy(n, 1).start()
 
@@ -567,9 +671,34 @@
         for n in range(3):
             w_copy(n, 1).wait_recv()
             w_copy(n, 2).wait_recv()
-            parts[n][4][...] = parts[n][1][0] + parts[n][3][1].astype(F32) + parts[n][3][2].astype(F32)
-
-    w_first()
+            parts[n][3][...] += parts[n][2][1].astype(F32) + parts[n][2][2].astype(F32)
+
+    def w_work(i):
+        @pl.when(i == 0)
+        def _():
+            load(chunks + 1).wait()
+            w_block(2)
+            for n in range(3):
+                w_copy(n, 0).start()
+
+        @pl.when(i == 1)
+        def _():
+            w_block(1)
+            w_copy(1, 2).start()
+
+        @pl.when(i == 2)
+        def _():
+            w_block(-1)
+            w_copy(0, 2).start()
+            w_copy(2, 2).start()
+
+        @pl.when(i == 4)
+        def _():
+            w_second()
+
+        @pl.when(i == 6)
+        def _():
+            w_block(0)
 
     def z_copy(k, direction, stage):
         sign = 1 - 2 * direction
@@ -630,17 +759,19 @@
             map_copy(s).start()
 
     def step(i, carry):
-        @pl.when((i >= 1) & (i < chunks))
-        def _():
-            y_start(i)
+        @pl.when(i + 2 < chunks)
+        def _():
+            y_start(i + 2)
 
         @pl.when((i >= 1) & (i <= chunks))
         def _():
             y_pass(i - 1)
 
-        @pl.when((i >= 3) & (i <= chunks + 2))
-        def _():
-            z_stage(i - 3, 2)
+        for stage in (1, 2, 3):
+
+            @pl.when((i >= 2 + stage) & (i < chunks + 2 + stage))
+            def _(stage=stage):
+                z_stage(i - 2 - stage, stage)
 
         @pl.when((i >= 2) & (i <= chunks + 1))
         def _():
@@ -650,37 +781,26 @@
             gbuf[k] = jnp.dot(spread[...], got, preferred_element_type=F32).reshape(NZ, rows, cw)
             z_stage(k, 0)
 
-        @pl.when((i >= 3) & (i <= chunks + 2))
-        def _():
-            z_stage(i - 3, 3)
-
-        @pl.when(i == 2)
+        @pl.when((i >= 6) & (i < chunks + 6))
+        def _():
+            z_finish(i - 6)
+
+        @pl.when(i == 3)
         def _():
             prob_grads()
 
-        @pl.when((i >= 2) & (i <= chunks + 1))
-        def _():
-            z_stage(i - 2, 1)
-
-        @pl.when((i >= 3) & (i <= chunks + 2))
-        def _():
-            z_finish(i - 3)
-
-        @pl.when(i == 3)
-        def _():
-            w_second()
-
+        w_work(i)
         return carry
 
-    lax.fori_loop(0, chunks + 3, step, 0)
+    lax.fori_loop(0, chunks + 6, step, 0)
     w_third()
     for s in range(1, NZ):
         z = mod(me.z - s, NZ)
         remote(maps.at[z], maps.at[z], map_send.at[s], map_recv.at[s], me.at_z(s)).wait_recv()
-    named = slots[...]
     given = maps[...].reshape(NZ * PLANE, rows)
-    for k in range(routes.shape[0]):
-        same = named == routes[k : k + 1, :]
+    wanted = routes[...].T
+    for k in range(wanted.shape[0]):
+        same = named[...] == wanted[k : k + 1, :]
         out_prob[k : k + 1, :] = jnp.sum(jnp.where(same, given, 0.0), axis=0, keepdims=True)
 
     def drain(k, carry):
@@ -703,13 +823,15 @@
             w_copy(n, hop).wait_send()
 
 
-def combine(dx, dp, key, routes, slots, part_gate, part_up, part_down, chunks=4):
-    _, _, width = dx.shape
+def combine(rows_in, wide, grads, dp, key, routes, slots):
+    total, _, _, cw = rows_in.shape
+    chunks = total // 2
+    width = chunks * cw
     rows = dp.shape[2]
-    cw = width // chunks
-    depth, ff = part_gate.shape[0] // NX, part_gate.shape[1]
+    depth, ff = wide.shape[0] // NX, wide.shape[1] // 2
     dma = pltpu.SemaphoreType.DMA
     vmem = pl.BlockSpec(memory_space=pltpu.VMEM)
+    smem = pl.BlockSpec(memory_space=pltpu.SMEM)
     anyp = pl.BlockSpec(memory_space=pl.ANY)
     shape = jax.ShapeDtypeStruct
     one, two = (depth, ff), (ff, width // NX)
@@ -717,12 +839,12 @@
         functools.partial(combine_kernel, width, chunks),
         out_shape=(
             shape((rows, width), BF16),
-            shape(routes.shape, F32),
+            shape(routes.shape[::-1], F32),
             shape(one, F32),
             shape(one, F32),
             shape(two, F32),
         ),
-        in_specs=[anyp, anyp, vmem, vmem, vmem, anyp, anyp, anyp],
+        in_specs=[anyp, anyp, anyp, anyp, vmem, vmem, smem],
         out_specs=(vmem, vmem, vmem, vmem, vmem),
         scratch_shapes=[
             pltpu.VMEM((chunks, PLANE, ROWS, cw), BF16),
@@ -735,9 +857,14 @@
             pltpu.VMEM((2, ROWS, rows), BF16),
             pltpu.VMEM((NZ, PLANE, rows), F32),
             pltpu.VMEM((NZ, PLANE, rows), F32),
-            pltpu.VMEM((NX,) + one, F32),
-            pltpu.VMEM((NX,) + one, F32),
-            pltpu.VMEM((NX,) + two, F32),
+            pltpu.VMEM(rows_in.shape, BF16),
+            pltpu.VMEM(wide.shape, BF16),
+            pltpu.VMEM(grads.shape, BF16),
+            pltpu.VMEM((chunks, PLANE, ROWS, cw), BF16),
+            pltpu.VMEM((NZ * PLANE, rows), jnp.int32),
+            pltpu.VMEM(one, F32),
+            pltpu.VMEM(one, F32),
+            pltpu.VMEM(two, F32),
             pltpu.VMEM((3,) + one, BF16),
             pltpu.VMEM((3,) + one, BF16),
             pltpu.VMEM((3,) + two, BF16),
@@ -754,57 +881,21 @@
             dma((chunks + 1,)),
             dma((3, 3)),
             dma((3, 3)),
-            dma((3, NX)),
+            dma((chunks + 2,)),
         ],
         compiler_params=pltpu.CompilerParams(
-            collective_id=1, has_side_effects=True, vmem_limit_bytes=62 * 1024 * 1024
+            collective_id=1, has_side_effects=True, vmem_limit_bytes=67043328
         ),
         name="combine",
-    )(dx, dp, key, routes, slots, part_gate, part_up, part_down)
+    )(rows_in, wide, grads, dp, key, routes, slots)
 
 
 def shards(tokens, cotangent, routes, probs, slot_expert, gate_w, up_w, down_w):
-    rows, width = tokens.shape
-    ff = gate_w.shape[2]
-    by_plane = slot_expert.reshape(NY, NZ, NC).transpose(1, 0, 2).reshape(-1)
-    slots = jnp.broadcast_to(by_plane[:, None], (by_plane.shape[0], rows))
-    turned = routes.T
-    x, dy, p, w_gate, w_up, w_down, key = dispatch(
-        tokens, cotangent, turned, probs.T.astype(F32), slots, gate_w[0], up_w[0], down_w[0]
+    rows_in, wide, grads, dp, key = dispatch(
+        tokens, cotangent, routes, probs, slot_expert, gate_w[0], up_w[0], down_w[0]
     )
-    total = PLANE * ROWS
-    x, dy = x.reshape(total, width), dy.reshape(total, width)
-    weight = p.reshape(total, rows)[:, :1].astype(F32)
-    w_gate, w_up = w_gate.reshape(width, ff), w_up.reshape(width, ff)
-    gate = jnp.dot(x, w_gate, preferred_element_type=F32)
-    upval = jnp.dot(x, w_up, preferred_element_type=F32)
-    sig = jax.nn.sigmoid(gate)
-    act = gate * sig
-    hidden = (act * upval).astype(BF16)
-    back = lax.dot_general(dy, w_down, (((1,), (1,)), ((), ())), preferred_element_type=F32)
-    dprob = jnp.sum(hidden.astype(F32) * back, axis=1, keepdims=True).astype(BF16)
-    dh = weight * back
-    d_gate = (dh * upval * sig * (1.0 + gate * (1.0 - sig))).astype(BF16)
-    d_up = (dh * act).astype(BF16)
-    wide = (((1,), (1,)), ((), ()))
-    dx = (
-        lax.dot_general(d_gate, w_gate, wide, preferred_element_type=F32)
-        + lax.dot_general(d_up, w_up, wide, preferred_element_type=F32)
-    ).astype(BF16)
-    wdy = (weight * dy.astype(F32)).astype(BF16)
-    tall = (((0,), (0,)), ((), ()))
-    part_gate = lax.dot_general(x, d_gate, tall, preferred_element_type=F32)
-    part_up = lax.dot_general(x, d_up, tall, preferred_element_type=F32)
-    part_down = lax.dot_general(hidden, wdy, tall, preferred_element_type=F32)
     grad_tokens, grad_probs, grad_gate, grad_up, grad_down = combine(
-        dx.reshape(PLANE, ROWS, width),
-        jnp.broadcast_to(dprob, (total, rows)).reshape(PLANE, ROWS, rows),
-        key,
-        turned,
-        slots,
-        part_gate,
-        part_up,
-        part_down,
+        rows_in, wide, grads, dp, key, routes, slot_expert
     )
     return (
         grad_tokens,

time: 296 us -> 254 us (0.86)
  matrix products: 41.4 us -> 0 us
    dot_general x8 -> x0, matrix products: 41.4 us -> none  [the longest x1 7.15 us: shards(): part_up = lax.dot_general(x, d_up, tall, preferred_element_type=F32)]
    pallas_call x1, Pallas kernels: 93.5 us -> 97.3 us  [combine(): pl.pallas_call(functools.partial(combine_kernel, width, chunks), out_shap...]
    pallas_call x1, Pallas kernels: 149 us -> 145 us  [dispatch(): pl.pallas_call(functools.partial(dispatch_kernel, width, chunks), out_sha...]
    unnamed x23 -> x10, local copies, waits for them, and re-layouts: 5.97 us -> 8.52 us
where the time goes in v2:
time: 254 us; the launch traced here: 253 us
  Pallas kernels  242 us (95%)
  local copies, waits for them, and re-layouts  8.52 us (3%)
    pallas_call x1, Pallas kernels, dispatch(): pl.pallas_call(functools.partial(dispatch_kernel, width, chunks), out_sha...  145 us
    pallas_call x1, Pallas kernels, combine(): pl.pallas_call(functools.partial(combine_kernel, width, chunks), out_shap...  97.3 us
    unnamed x10, local copies, waits for them, and re-layouts  8.52 us

profile of v2, /device:TPU:32, one launch (start us, length us, event | category | flops | bytes accessed | tf_op | source)
XLA Modules:
  0.0 252.9 jit_solution(345049953577044733)
XLA Ops:
  0.6 1.4 copy.14.probs
  2.0 1.4 copy.13.routes
  3.4 145.0 %dispatch.1 = (bf16[16,8,144,256]{3,2,1,0:T(8,128)(2,1)}, bf16[2048,768]{1,0:T(8,128)(2,1)}, bf16[1152,1152]{1,0:T(8,128)(2,1)}, bf16[8,144,128]{2,1,0:T(8,128)(2,1)}, f32[8,1024]{1,0:T(8,128)}) custom-call(bf16[128,2048]{1,0:T(8,128)(2,1)} %tok.1, bf16[128,2048]{1,0:T(8,128)(2,1)} %cot.1, s32[128,8]{1,0:T(8,128)} %copy.13.routes, ...), custom_call_target="tpu_custom_call" | custom-call | tf_op jit(solution)/shard_map/dispatch/pallas_call | solution.py:453
  148.4 97.3 %combine.1 = (bf16[128,2048]{1,0:T(8,128)(2,1)}, f32[8,128]{1,0:T(8,128)}, f32[512,384]{1,0:T(8,128)}, f32[512,384]{1,0:T(8,128)}, f32[384,512]{1,0:T(8,128)}) custom-call(bf16[16,8,144,256]{3,2,1,0:T(8,128)(2,1)} %get-tuple-element.15.rows_in, bf16[2048,768]{1,0:T(8,128)(2,1)} %get-tuple-element.16.wide_in, bf16[1152,1152]{1,0:T(8,128)(2,1)} %get-tuple-element.17.grads_in, ...), custom_call_target="tpu_custom_call" | custom-call | tf_op jit(solution)/shard_map/combine/pallas_call | solution.py:838
  245.8 0.0 copy-start.1
  245.8 0.0 copy-start
  245.8 1.4 convert_bitcast_fusion
  247.2 1.9 copy.20
  249.1 2.1 copy.21
  251.1 0.0 copy-done.1
  251.1 0.9 copy.22
  252.0 0.0 copy-done
  252.0 0.9 copy.23
Async XLA Ops:
  245.8 5.3 %copy-start.1 = (f32[512,384]{1,0:T(8,128)S(1)}, f32[512,384]{1,0:T(8,128)}, u32[]{:S(2)}) copy-start(f32[512,384]{1,0:T(8,128)} %get-tuple-element.23) | copy-start | bytes 2359300
  245.8 6.2 %copy-start = (f32[384,512]{1,0:T(8,128)S(1)}, f32[384,512]{1,0:T(8,128)}, u32[]{:S(2)}) copy-start(f32[384,512]{1,0:T(8,128)} %get-tuple-element.24) | copy-start | bytes 2359300

commit v3 on v2

--- a/solution.py
+++ b/solution.py
@@ -12,6 +12,8 @@
 PLANE = NY * NC
 ROWS = NZ * CAP
 LAG = 8
+W_PASS = 9
+W_USE = 14
 MESH = pl.DeviceIdType.MESH
 F32 = jnp.float32
 BF16 = jnp.bfloat16
@@ -44,17 +46,37 @@
 
     def peers(self):
         out = [self.at_z(s) for s in range(1, NZ)]
-        out += [self.at_y(s, c) for s in (1, -1) for c in range(NC)]
+        out += [self.at_y(s, c) for s in (1, 2, 3) for c in range(NC)]
         out += [self.at_y(0, 1 - self.c), self.at_x(1), self.at_x(-1)]
         return out
 
 
-def greet(me):
-    barrier = pltpu.get_barrier_semaphore()
-    peers = me.peers()
-    for peer in peers:
-        pl.semaphore_signal(barrier, inc=1, device_id=peer, device_id_type=MESH)
-    pl.semaphore_wait(barrier, len(peers))
+def hail(me):
+    for peer in me.peers():
+        pl.semaphore_signal(pltpu.get_barrier_semaphore(), inc=1, device_id=peer, device_id_type=MESH)
+
+
+def met(me):
+    pl.semaphore_wait(pltpu.get_barrier_semaphore(), len(me.peers()))
+
+
+def diagonal(count, lanes):
+    down = lax.broadcasted_iota(jnp.int32, (count, lanes), 0)
+    return down == lax.broadcasted_iota(jnp.int32, (count, lanes), 1)
+
+
+def fold(column, lanes):
+    rest = ROWS - lanes
+    first = jnp.sum(jnp.where(diagonal(lanes, lanes), column[:lanes], 0.0), axis=0, keepdims=True)
+    second = jnp.sum(jnp.where(diagonal(rest, lanes), column[lanes:], 0.0), axis=0, keepdims=True)
+    return jnp.concatenate([first, second, jnp.zeros((6, lanes), F32)], axis=0)
+
+
+def unfold(tile):
+    lanes = tile.shape[1]
+    first = jnp.sum(jnp.where(diagonal(lanes, lanes), tile[0:1], 0.0), axis=1, keepdims=True)
+    second = jnp.sum(jnp.where(diagonal(ROWS - lanes, lanes), tile[1:2], 0.0), axis=1, keepdims=True)
+    return jnp.broadcast_to(jnp.concatenate([first, second], axis=0), (ROWS, lanes))
 
 
 def remote(src, dst, send, recv, dev):
@@ -63,23 +85,12 @@
     )
 
 
-def plane_send(me, piece, landing, relay, send, recv, relay_recv):
-    for step, core in ((1, 0), (-1, 1)):
-        remote(
-            piece(mod(me.y + 2, NY) * NC + core), relay(core), send, relay_recv(core), me.at_y(step, me.c)
-        ).start()
-    for step in (1, -1):
+def plane_send(me, piece, landing, send, recv):
+    for step in (2, 1, -1):
         for core in range(NC):
             there = mod(me.y + step, NY)
             remote(piece(there * NC + core), landing(me.plane), send, recv, me.at_y(step, core)).start()
     remote(piece(me.y * NC + 1 - me.c), landing(me.plane), send, recv, me.at_y(0, 1 - me.c)).start()
-
-
-def plane_relay(me, landing, relay, send, recv, relay_recv):
-    for step, core in ((1, 0), (-1, 1)):
-        remote(relay(core), relay(core), send, relay_recv(core), me.at_y(step, core)).wait_recv()
-        origin = mod(me.y - step, NY) * NC + me.c
-        remote(relay(core), landing(origin), send, recv, me.at_y(step, core)).start()
 
 
 def slot_rows(slot_expert, named):
@@ -108,7 +119,6 @@
     key_out,
     zbuf,
     sbuf,
-    relay,
     landed,
     wide,
     tall,
@@ -117,12 +127,12 @@
     grads,
     dp,
     pin,
+    share_of,
     named,
     maps_own,
     maps,
     pick,
     pbuf,
-    prelay,
     own_sem,
     map_send,
     map_recv,
@@ -130,7 +140,6 @@
     z_recv,
     y_send,
     y_recv,
-    r_recv,
     y_own,
     w_send,
     w_recv,
@@ -145,6 +154,8 @@
     total = 2 * chunks
     rows = tok.shape[0]
 
+    hail(me)
+
     def own_copy(k):
         src = (tok, cot)[k // chunks]
         return pltpu.make_async_copy(
@@ -157,8 +168,8 @@
     hit = jnp.zeros((NZ * PLANE, rows), F32)
     weight = jnp.zeros((NZ * PLANE, rows), F32)
     slot_rows(slots, named)
-    turned = routes[...].T
-    shares = probs[...].astype(F32).T
+    turned = routes[...]
+    shares = probs[...].astype(F32)
     for k in range(turned.shape[0]):
         same = named[...] == turned[k : k + 1, :]
         hit = hit + jnp.where(same, 1.0, 0.0)
@@ -177,7 +188,7 @@
     for k in range(total):
         own_copy(k).wait()
 
-    greet(me)
+    met(me)
 
     def z_copy(k, direction, stage):
         sign = 1 - 2 * direction
@@ -240,31 +251,21 @@
             w_copy(n, direction, 0).start()
         pltpu.make_async_copy(weights[n], w_slot(n, me.x), w_own.at[n]).start()
 
-    for s in range(1, NZ):
-        z = mod(me.z - s, NZ)
-        remote(maps.at[z], maps.at[z], map_send.at[s], map_recv.at[s], me.at_z(s)).wait_recv()
-    row = lax.broadcasted_iota(jnp.int32, (ROWS, rows), 0).astype(F32)
-    ones = jnp.ones((rows, rows), BF16)
-    for d in range(PLANE):
+    def choose(d):
+        row = lax.broadcasted_iota(jnp.int32, (ROWS, rows), 0).astype(F32)
         share = jnp.zeros((ROWS, rows), F32)
         for z in range(NZ):
             taken = maps[z, 0, d : d + 1, :] == row
             pick[d * ROWS : (d + 1) * ROWS, z * rows : (z + 1) * rows] = jnp.where(taken, 1.0, 0.0).astype(BF16)
             share = share + jnp.where(taken, maps[z, 1, d : d + 1, :], 0.0)
             key_out[d : d + 1, z * rows : (z + 1) * rows] = maps[z, 0, d : d + 1, :]
-        pbuf[d] = jnp.dot(share.astype(BF16), ones, preferred_element_type=F32).astype(BF16)
+        pbuf[d] = fold(jnp.sum(share, axis=1, keepdims=True), rows)
 
     last = total
 
     def piece(k):
         return lambda d: sbuf.at[k, d]
 
-    def relay_of(k):
-        return lambda core: relay.at[k, core]
-
-    def relay_sem(k):
-        return lambda core: r_recv.at[k, core]
-
     def landing(k):
         return lambda slot: landed.at[k, slot]
 
@@ -272,11 +273,8 @@
         return pltpu.make_async_copy(sbuf.at[k, me.plane], landed.at[k, me.plane], y_own.at[k])
 
     def send_chunk(k):
-        plane_send(me, piece(k), landing(k), relay_of(k), y_send.at[k], y_recv.at[k], relay_sem(k))
+        plane_send(me, piece(k), landing(k), y_send.at[k], y_recv.at[k])
         own_rows(k).start()
-
-    def relay_chunk(k):
-        plane_relay(me, landing(k), relay_of(k), y_send.at[k], y_recv.at[k], relay_sem(k))
 
     def seven_of(k):
         sent, here = sbuf.at[k, pl.ds(0, PLANE - 1)], landed.at[k, pl.ds(0, PLANE - 1)]
@@ -285,45 +283,32 @@
     def rows_out(k):
         return pltpu.make_async_copy(landed.at[k], out_rows.at[k], out_sem.at[k])
 
-    def consume(k):
+    def consume_x(k):
         seven_of(k).wait_recv()
         own_rows(k).wait()
-
-        @pl.when(k < chunks)
-        def _():
-            take = pl.ds(pl.multiple_of(k * cw, cw), cw)
-            acc[...] += jnp.dot(
-                landed[k].reshape(PLANE * ROWS, cw), wide[take, :], preferred_element_type=F32
-            )
-
-        @pl.when(k >= chunks)
-        def _():
-            take = pl.ds(pl.multiple_of((k - chunks) * cw, cw), cw)
-            racc[...] += lax.dot_general(
-                landed[k].reshape(PLANE * ROWS, cw),
-                tall[:, take],
-                (((1,), (1,)), ((), ())),
-                preferred_element_type=F32,
-            )
-            for d in range(PLANE):
-                for j in range(cw // rows):
-                    part = slice(j * rows, (j + 1) * rows)
-                    scaled = landed[k, d, :, part].astype(F32) * pin[d].astype(F32)
-                    landed[k, d, :, part] = scaled.astype(BF16)
-
+        take = pl.ds(pl.multiple_of(k * cw, cw), cw)
+        acc[...] += jnp.dot(landed[k].reshape(PLANE * ROWS, cw), wide[take, :], preferred_element_type=F32)
+        rows_out(k).start()
+
+    def consume_dy(k):
+        seven_of(k).wait_recv()
+        own_rows(k).wait()
+        take = pl.ds(pl.multiple_of((k - chunks) * cw, cw), cw)
+        racc[...] += lax.dot_general(
+            landed[k].reshape(PLANE * ROWS, cw),
+            tall[:, take],
+            (((1,), (1,)), ((), ())),
+            preferred_element_type=F32,
+        )
+        for d in range(PLANE):
+            for j in range(cw // rows):
+                part = slice(j * rows, (j + 1) * rows)
+                scaled = landed[k, d, :, part].astype(F32) * share_of[d]
+                landed[k, d, :, part] = scaled.astype(BF16)
         rows_out(k).start()
 
     def p_land(slot):
         return pin.at[slot]
-
-    def p_relay(core):
-        return prelay.at[core]
-
-    def p_sem(core):
-        return r_recv.at[last, core]
-
-    acc[...] = jnp.zeros_like(acc)
-    racc[...] = jnp.zeros_like(racc)
 
     def wide_out(n):
         if n == 0:
@@ -335,16 +320,6 @@
         return remote(sent, here, y_send.at[last], y_recv.at[last], me.at_y(1, 0))
 
     def step(i, carry):
-        @pl.when((i >= 1) & (i < total))
-        def _():
-            z_stage(i, 0)
-
-        for stage in (1, 2, 3):
-
-            @pl.when((i >= stage) & (i < total + stage))
-            def _(stage=stage):
-                z_stage(i - stage, stage)
-
         @pl.when((i >= 4) & (i < total + 4))
         def _():
             k = i - 4
@@ -354,41 +329,64 @@
             sbuf[k] = out.reshape(PLANE, ROWS, cw)
             send_chunk(k)
 
-        @pl.when((i >= 6) & (i < total + 6))
-        def _():
-            relay_chunk(i - 6)
-
-        @pl.when(i == 5)
+        for stage in (3, 2, 1):
+
+            @pl.when((i >= stage) & (i < total + stage))
+            def _(stage=stage):
+                z_stage(i - stage, stage)
+
+        @pl.when((i >= 1) & (i < total))
+        def _():
+            z_stage(i, 0)
+
+        @pl.when(i == 0)
+        def _():
+            for s in range(1, NZ):
+                z = mod(me.z - s, NZ)
+                remote(maps.at[z], maps.at[z], map_send.at[s], map_recv.at[s], me.at_z(s)).wait_recv()
+
+        for turn in range(4):
+
+            @pl.when(i == turn)
+            def _(turn=turn):
+                choose(2 * turn)
+                choose(2 * turn + 1)
+
+        @pl.when(i == 6)
+        def _():
+            acc[...] = jnp.zeros_like(acc)
+            racc[...] = jnp.zeros_like(racc)
+
+        @pl.when(i == 4)
+        def _():
+            plane_send(me, lambda d: pbuf.at[d], p_land, y_send.at[last], y_recv.at[last])
+            pltpu.make_async_copy(pbuf.at[me.plane], pin.at[me.plane], y_own.at[last]).start()
+
+        @pl.when(i == W_PASS)
         def _():
             for n in range(3):
                 for direction in (0, 1):
                     w_wait(n, direction, 0)
                 w_copy(n, 0 if n < 2 else 1, 1).start()
 
-        @pl.when(i == 6)
-        def _():
-            plane_send(me, lambda d: pbuf.at[d], p_land, p_relay, y_send.at[last], y_recv.at[last], p_sem)
-            pltpu.make_async_copy(pbuf.at[me.plane], pin.at[me.plane], y_own.at[last]).start()
-
-        @pl.when(i == 8)
-        def _():
-            plane_relay(me, p_land, p_relay, y_send.at[last], y_recv.at[last], p_sem)
-
-        @pl.when(i == LAG)
+        @pl.when(i == W_USE)
         def _():
             for n in range(3):
                 w_wait(n, 0 if n < 2 else 1, 1)
                 pltpu.make_async_copy(weights[n], w_slot(n, me.x), w_own.at[n]).wait()
             wide_out(0).start()
-
-        @pl.when(i == chunks + LAG)
-        def _():
             p_seven().wait_recv()
             pltpu.make_async_copy(pbuf.at[me.plane], pin.at[me.plane], y_own.at[last]).wait()
-
-        @pl.when((i >= LAG) & (i < total + LAG))
-        def _():
-            consume(i - LAG)
+            for d in range(PLANE):
+                share_of[d] = unfold(pin[d])
+
+        @pl.when((i >= W_USE) & (i < chunks + W_USE))
+        def _():
+            consume_x(i - W_USE)
+
+        @pl.when((i >= chunks + LAG) & (i < total + LAG))
+        def _():
+            consume_dy(i - LAG)
 
         return carry
 
@@ -397,13 +395,13 @@
     def point(d, carry):
         these = pl.ds(pl.multiple_of(d * ROWS, 16), ROWS)
         g, u, r = acc[these, :ff], acc[these, ff:], racc[these, :]
-        p = pin[d].astype(F32)
+        p = share_of[d]
         p = jnp.concatenate([p] * (ff // rows), axis=1)
         sg = jax.nn.sigmoid(g)
         act = g * sg
         hidden = (act * u).astype(BF16)
         given = jnp.sum(hidden.astype(F32) * r, axis=1, keepdims=True)
-        dp[d] = jnp.broadcast_to(given, (ROWS, rows)).astype(BF16)
+        dp[d] = fold(given.astype(BF16).astype(F32), rows)
         dh = p * r
         grads[these, :ff] = (dh * u * sg * (1.0 + g * (1.0 - sg))).astype(BF16)
         grads[these, ff : 2 * ff] = (dh * act).astype(BF16)
@@ -428,15 +426,11 @@
             for stage in range(4):
                 z_copy(k, direction, stage).wait_send()
         seven_of(k).wait_send()
-        two = sbuf.at[k, pl.ds(0, 2)]
-        remote(two, two, y_send.at[k], y_recv.at[k], me.at_y(1, 0)).wait_send()
         rows_out(k).wait()
         return carry
 
     lax.fori_loop(0, total, drain, 0)
-    two = pbuf.at[pl.ds(0, 2)]
     p_seven().wait_send()
-    remote(two, two, y_send.at[last], y_recv.at[last], me.at_y(1, 0)).wait_send()
     wide_out(0).wait()
     wide_out(1).wait()
     dp_out.wait()
@@ -456,7 +450,7 @@
             shape((total, PLANE, ROWS, cw), BF16),
             shape((NX * depth, 2 * ff), BF16),
             shape((PLANE * ROWS, 3 * ff), BF16),
-            shape((PLANE, ROWS, rows), BF16),
+            shape((PLANE, 8, rows), F32),
             shape((PLANE, NZ * rows), F32),
         ),
         in_specs=[anyp, anyp, vmem, vmem, pl.BlockSpec(memory_space=pltpu.SMEM), vmem, vmem, vmem],
@@ -464,21 +458,20 @@
         scratch_shapes=[
             pltpu.VMEM((total, NZ, rows, cw), BF16),
             pltpu.VMEM((total, PLANE, ROWS, cw), BF16),
-            pltpu.VMEM((total, 2, ROWS, cw), BF16),
             pltpu.VMEM((total, PLANE, ROWS, cw), BF16),
             pltpu.VMEM((NX * depth, 2 * ff), BF16),
             pltpu.VMEM((ff, width), BF16),
             pltpu.VMEM((PLANE * ROWS, 2 * ff), F32),
             pltpu.VMEM((PLANE * ROWS, ff), F32),
             pltpu.VMEM((PLANE * ROWS, 3 * ff), BF16),
-            pltpu.VMEM((PLANE, ROWS, rows), BF16),
-            pltpu.VMEM((PLANE, ROWS, rows), BF16),
+            pltpu.VMEM((PLANE, 8, rows), F32),
+            pltpu.VMEM((PLANE, 8, rows), F32),
+            pltpu.VMEM((PLANE, ROWS, rows), F32),
             pltpu.VMEM((NZ * PLANE, rows), jnp.int32),
             pltpu.VMEM((NZ, 2, PLANE, rows), F32),
             pltpu.VMEM((NZ, 2, PLANE, rows), F32),
             pltpu.VMEM((PLANE * ROWS, NZ * rows), BF16),
-            pltpu.VMEM((PLANE, ROWS, rows), BF16),
-            pltpu.VMEM((2, ROWS, rows), BF16),
+            pltpu.VMEM((PLANE, 8, rows), F32),
             dma((total,)),
             dma((NZ,)),
             dma((NZ,)),
@@ -486,7 +479,6 @@
             dma((total, 2, 4)),
             dma((total + 1,)),
             dma((total + 1,)),
-            dma((total + 1, 2)),
             dma((total + 1,)),
             dma((3, 2, 2)),
             dma((3, 2, 2)),
@@ -516,13 +508,11 @@
     out_up,
     out_down,
     rbuf,
-    relay,
     spread,
     gbuf,
     zout,
     zin,
     pbuf,
-    prelay,
     maps_own,
     maps,
     kept,
@@ -545,11 +535,14 @@
     z_recv,
     y_send,
     y_recv,
-    r_recv,
     y_own,
     w_send,
     w_recv,
+    own0,
+    own1,
+    own2,
     load_sem,
+    w_out,
 ):
     me = Place()
     cw = width // chunks
@@ -558,7 +551,8 @@
     per = width // NX // cw
     rows = out_tok.shape[0]
     last = chunks
-    parts = ((wmid0, wout0, win0, out_gate), (wmid1, wout1, win1, out_up), (wmid2, wout2, win2, out_down))
+    parts = ((wmid0, wout0, win0, own0), (wmid1, wout1, win1, own1), (wmid2, wout2, win2, own2))
+    finals = (out_gate, out_up, out_down)
     way = (1, -1, 1)
 
     def load(n):
@@ -569,10 +563,43 @@
             return pltpu.make_async_copy(grads_in, grads, load_sem.at[n])
         return pltpu.make_async_copy(rows_in, kept, load_sem.at[n])
 
+    hail(me)
     load(chunks).start()
     for n in range(chunks):
         load(n).start()
     load(chunks + 1).start()
+
+    met(me)
+
+    def cols(k):
+        return pl.ds(pl.multiple_of(k * cw, cw), cw)
+
+    def piece(k):
+        return lambda d: dx.at[k, d]
+
+    def landing(k):
+        return lambda slot: rbuf.at[k, slot]
+
+    def y_start(k):
+        out = lax.dot_general(
+            grads[:, : 2 * ff], wide[cols(k), :], (((1,), (1,)), ((), ())), preferred_element_type=F32
+        )
+        dx[k] = out.astype(BF16).reshape(PLANE, ROWS, cw)
+        plane_send(me, piece(k), landing(k), y_send.at[k], y_recv.at[k])
+        pltpu.make_async_copy(piece(k)(me.plane), rbuf.at[k, me.plane], y_own.at[k]).start()
+
+    def p_land(slot):
+        return pbuf.at[slot]
+
+    plane_send(me, lambda d: dp.at[d], p_land, y_send.at[last], y_recv.at[last])
+    pltpu.make_async_copy(dp.at[me.plane], pbuf.at[me.plane], y_own.at[last]).start()
+    load(chunks).wait()
+    load(0).wait()
+    y_start(0)
+    load(1).wait()
+    y_start(1)
+    for n in range(2, chunks):
+        load(n).wait()
     slot_rows(slots, named)
 
     lane = lax.broadcasted_iota(jnp.int32, (NZ * rows, 128), 1).astype(F32)
@@ -584,52 +611,6 @@
             where = jnp.where(mine >= 0.0, mine + float(d * ROWS - 128 * j), -1.0)
             tile = tile + jnp.where(where == lane, 1.0, 0.0)
         spread[:, j * 128 : (j + 1) * 128] = tile.astype(BF16)
-
-    greet(me)
-
-    def cols(k):
-        return pl.ds(pl.multiple_of(k * cw, cw), cw)
-
-    def piece(k):
-        return lambda d: dx.at[k, d]
-
-    def landing(k):
-        return lambda slot: rbuf.at[k, slot]
-
-    def relay_of(k):
-        return lambda core: relay.at[k, core]
-
-    def relay_sem(k):
-        return lambda core: r_recv.at[k, core]
-
-    def y_start(k):
-        out = lax.dot_general(
-            grads[:, : 2 * ff], wide[cols(k), :], (((1,), (1,)), ((), ())), preferred_element_type=F32
-        )
-        dx[k] = out.astype(BF16).reshape(PLANE, ROWS, cw)
-        plane_send(me, piece(k), landing(k), relay_of(k), y_send.at[k], y_recv.at[k], relay_sem(k))
-        pltpu.make_async_copy(piece(k)(me.plane), rbuf.at[k, me.plane], y_own.at[k]).start()
-
-    def y_pass(k):
-        plane_relay(me, landing(k), relay_of(k), y_send.at[k], y_recv.at[k], relay_sem(k))
-
-    def p_land(slot):
-        return pbuf.at[slot]
-
-    def p_relay(core):
-        return prelay.at[core]
-
-    def p_sem(core):
-        return r_recv.at[last, core]
-
-    plane_send(me, lambda d: dp.at[d], p_land, p_relay, y_send.at[last], y_recv.at[last], p_sem)
-    pltpu.make_async_copy(dp.at[me.plane], pbuf.at[me.plane], y_own.at[last]).start()
-    load(chunks).wait()
-    for n in range(chunks):
-        load(n).wait()
-    y_start(0)
-    y_start(1)
-    plane_relay(me, p_land, p_relay, y_send.at[last], y_recv.at[last], p_sem)
 
     def w_copy(n, hop):
         sign = way[n] if hop < 2 else -way[n]
@@ -672,6 +653,7 @@
             w_copy(n, 1).wait_recv()
             w_copy(n, 2).wait_recv()
             parts[n][3][...] += parts[n][2][1].astype(F32) + parts[n][2][2].astype(F32)
+            pltpu.make_async_copy(parts[n][3], finals[n], w_out.at[n]).start()
 
     def w_work(i):
         @pl.when(i == 0)
@@ -699,6 +681,10 @@
         @pl.when(i == 6)
         def _():
             w_block(0)
+
+        @pl.when(i == chunks + 3)
+        def _():
+            w_third()
 
     def z_copy(k, direction, stage):
         sign = 1 - 2 * direction
@@ -750,7 +736,7 @@
         pltpu.make_async_copy(dp.at[me.plane], pbuf.at[me.plane], y_own.at[last]).wait()
         row = lax.broadcasted_iota(jnp.int32, (ROWS, rows), 0).astype(F32)
         for d in range(PLANE):
-            given = pbuf[d].astype(F32)
+            given = unfold(pbuf[d])
             for z in range(NZ):
                 taken = key[d : d + 1, z * rows : (z + 1) * rows] == row
                 maps_own[z, d : d + 1, :] = jnp.sum(jnp.where(taken, given, 0.0), axis=0, keepdims=True)
@@ -763,10 +749,6 @@
         def _():
             y_start(i + 2)
 
-        @pl.when((i >= 1) & (i <= chunks))
-        def _():
-            y_pass(i - 1)
-
         for stage in (1, 2, 3):
 
             @pl.when((i >= 2 + stage) & (i < chunks + 2 + stage))
@@ -793,34 +775,34 @@
         return carry
 
     lax.fori_loop(0, chunks + 6, step, 0)
-    w_third()
     for s in range(1, NZ):
         z = mod(me.z - s, NZ)
         remote(maps.at[z], maps.at[z], map_send.at[s], map_recv.at[s], me.at_z(s)).wait_recv()
     given = maps[...].reshape(NZ * PLANE, rows)
-    wanted = routes[...].T
+    wanted = routes[...]
+    found = []
     for k in range(wanted.shape[0]):
         same = named[...] == wanted[k : k + 1, :]
-        out_prob[k : k + 1, :] = jnp.sum(jnp.where(same, given, 0.0), axis=0, keepdims=True)
+        found.append(jnp.sum(jnp.where(same, given, 0.0), axis=0, keepdims=True))
+    out_prob[...] = jnp.concatenate(found, axis=0).astype(BF16)
 
     def drain(k, carry):
         for direction in (0, 1):
             for stage in range(4):
                 z_copy(k, direction, stage).wait_send()
-        seven, two = rbuf.at[k, pl.ds(0, PLANE - 1)], rbuf.at[k, pl.ds(0, 2)]
+        seven = rbuf.at[k, pl.ds(0, PLANE - 1)]
         remote(seven, seven, y_send.at[k], y_recv.at[k], me.at_y(1, 0)).wait_send()
-        remote(two, two, y_send.at[k], y_recv.at[k], me.at_y(1, 0)).wait_send()
         return carry
 
     lax.fori_loop(0, chunks, drain, 0)
-    seven, two = pbuf.at[pl.ds(0, PLANE - 1)], pbuf.at[pl.ds(0, 2)]
+    seven = pbuf.at[pl.ds(0, PLANE - 1)]
     remote(seven, seven, y_send.at[last], y_recv.at[last], me.at_y(1, 0)).wait_send()
-    remote(two, two, y_send.at[last], y_recv.at[last], me.at_y(1, 0)).wait_send()
     for s in range(1, NZ):
         map_copy(s).wait_send()
     for n in range(3):
         for hop in range(3):
             w_copy(n, hop).wait_send()
+        pltpu.make_async_copy(parts[n][3], finals[n], w_out.at[n]).wait()
 
 
 def combine(rows_in, wide, grads, dp, key, routes, slots):
@@ -839,22 +821,20 @@
         functools.partial(combine_kernel, width, chunks),
         out_shape=(
             shape((rows, width), BF16),
-            shape(routes.shape[::-1], F32),
+            shape(routes.shape, BF16),
             shape(one, F32),
             shape(one, F32),
             shape(two, F32),
         ),
         in_specs=[anyp, anyp, anyp, anyp, vmem, vmem, smem],
-        out_specs=(vmem, vmem, vmem, vmem, vmem),
+        out_specs=(vmem, vmem, anyp, anyp, anyp),
         scratch_shapes=[
             pltpu.VMEM((chunks, PLANE, ROWS, cw), BF16),
-            pltpu.VMEM((chunks, 2, ROWS, cw), BF16),
             pltpu.VMEM((NZ * rows, PLANE * ROWS), BF16),
             pltpu.VMEM((chunks, NZ, rows, cw), F32),
             pltpu.VMEM((chunks, 2, 4, rows, cw), BF16),
             pltpu.VMEM((chunks, 2, 4, rows, cw), BF16),
-            pltpu.VMEM((PLANE, ROWS, rows), BF16),
-            pltpu.VMEM((2, ROWS, rows), BF16),
+            pltpu.VMEM((PLANE, 8, rows), F32),
             pltpu.VMEM((NZ, PLANE, rows), F32),
             pltpu.VMEM((NZ, PLANE, rows), F32),
             pltpu.VMEM(rows_in.shape, BF16),
@@ -877,11 +857,14 @@
             dma((chunks, 2, 4)),
             dma((chunks + 1,)),
             dma((chunks + 1,)),
-            dma((chunks + 1, 2)),
             dma((chunks + 1,)),
             dma((3, 3)),
             dma((3, 3)),
+            pltpu.VMEM(one, F32),
+            pltpu.VMEM(one, F32),
+            pltpu.VMEM(two, F32),
             dma((chunks + 2,)),
+            dma((3,)),
         ],
         compiler_params=pltpu.CompilerParams(
             collective_id=1, has_side_effects=True, vmem_limit_bytes=67043328
@@ -890,16 +873,40 @@
     )(rows_in, wide, grads, dp, key, routes, slots)
 
 
+def hand_over_kernel(*refs):
+    half = len(refs) // 2
+    for src, dst in zip(refs[:half], refs[half:]):
+        dst[...] = src[...]
+
+
+def hand_over(*arrays, steps=4):
+    specs = []
+    for array in arrays:
+        count = array.shape[0]
+        if count >= 8 * steps:
+            specs.append(pl.BlockSpec((count // steps, array.shape[1]), lambda i: (i, 0)))
+        else:
+            specs.append(pl.BlockSpec(array.shape, lambda i: (0, 0)))
+    return pl.pallas_call(
+        hand_over_kernel,
+        grid=(steps,),
+        out_shape=tuple(jax.ShapeDtypeStruct(array.shape, array.dtype) for array in arrays),
+        in_specs=specs,
+        out_specs=tuple(specs),
+        name="hand_over",
+    )(*arrays)
+
+
 def shards(tokens, cotangent, routes, probs, slot_expert, gate_w, up_w, down_w):
     rows_in, wide, grads, dp, key = dispatch(
-        tokens, cotangent, routes, probs, slot_expert, gate_w[0], up_w[0], down_w[0]
+        tokens, cotangent, routes.T, probs.T, slot_expert, gate_w[0], up_w[0], down_w[0]
     )
-    grad_tokens, grad_probs, grad_gate, grad_up, grad_down = combine(
-        rows_in, wide, grads, dp, key, routes, slot_expert
+    grad_tokens, grad_probs, grad_gate, grad_up, grad_down = hand_over(
+        *combine(rows_in, wide, grads, dp, key, routes.T, slot_expert)
     )
     return (
         grad_tokens,
-        grad_probs.T.astype(BF16),
+        grad_probs.T,
         grad_gate[None],
         grad_up[None],
         grad_down[None],

time: 254 us -> 222 us (0.87)
  Pallas kernels: 242 us -> 221 us
  local copies, waits for them, and re-layouts: 8.52 us -> 0 us
    pallas_call x1, Pallas kernels: 97.3 us -> 82.2 us  [combine(): pl.pallas_call(functools.partial(combine_kernel, width, chunks), out_shap...]
    pallas_call x1, Pallas kernels: 145 us -> 134 us  [dispatch(): pl.pallas_call(functools.partial(dispatch_kernel, width, chunks), out_sha...]
    unnamed x10 -> x0, local copies, waits for them, and re-layouts: 8.52 us -> none
    pallas_call x0 -> x1, Pallas kernels: none -> 4.14 us  [hand_over(): pl.pallas_call(hand_over_kernel, grid=(steps,), out_shape=tuple((jax.Shap...]
where the time goes in v3:
time: 222 us; the launch traced here: 221 us
  Pallas kernels  221 us (100%)
    pallas_call x1, Pallas kernels, dispatch(): pl.pallas_call(functools.partial(dispatch_kernel, width, chunks), out_sha...  134 us
    pallas_call x1, Pallas kernels, combine(): pl.pallas_call(functools.partial(combine_kernel, width, chunks), out_shap...  82.2 us

profile of v3, /device:TPU:32, one launch (start us, length us, event | category | flops | bytes accessed | tf_op | source)
XLA Modules:
  0.0 221.3 jit_solution(10394847713518258271)
XLA Ops:
  0.6 134.3 %dispatch.1 = (bf16[16,8,144,256]{3,2,1,0:T(8,128)(2,1)}, bf16[2048,768]{1,0:T(8,128)(2,1)}, bf16[1152,1152]{1,0:T(8,128)(2,1)}, f32[8,8,128]{2,1,0:T(8,128)}, f32[8,1024]{1,0:T(8,128)}) custom-call(bf16[128,2048]{1,0:T(8,128)(2,1)} %tok.1, bf16[128,2048]{1,0:T(8,128)(2,1)} %cot.1, s32[8,128]{1,0:T(8,128)} %bitcast.12, bf16[8,128]{1,0:T(8,128)(2,1)} %bitcast.14, ...), custom_call_target="tpu_custom_call" | custom-call | tf_op jit(solution)/shard_map/dispatch/pallas_call | solution.py:447
  134.9 82.2 %combine.1 = (bf16[128,2048]{1,0:T(8,128)(2,1)}, bf16[8,128]{1,0:T(8,128)(2,1)}, f32[512,384]{1,0:T(8,128)}, f32[512,384]{1,0:T(8,128)}, f32[384,512]{1,0:T(8,128)}) custom-call(bf16[16,8,144,256]{3,2,1,0:T(8,128)(2,1)} %get-tuple-element.20.rows_in, bf16[2048,768]{1,0:T(8,128)(2,1)} %get-tuple-element.21.wide_in, ...), custom_call_target="tpu_custom_call" | custom-call | tf_op jit(solution)/shard_map/combine/pallas_call | solution.py:820
  217.1 4.1 %hand_over.1 = (bf16[128,2048]{1,0:T(8,128)(2,1)}, bf16[8,128]{1,0:T(8,128)(2,1)}, f32[512,384]{1,0:T(8,128)}, f32[512,384]{1,0:T(8,128)}, f32[384,512]{1,0:T(8,128)}) custom-call(bf16[128,2048]{1,0:T(8,128)(2,1)} %get-tuple-element.25.refs_0_, bf16[8,128]{1,0:T(8,128)(2,1)} %get-tuple-element.26.refs_1_, f32[512,384]{1,0:T(8,128)} %get-tuple-element.27.refs_2_, ...), custom_call_target="tpu_custom_call" | custom-call | tf_op jit(solution)/shard_map/hand_over/pallas_call | solution.py:890

commit v4 on v3

--- a/solution.py
+++ b/solution.py
@@ -406,11 +406,11 @@
         grads[these, :ff] = (dh * u * sg * (1.0 + g * (1.0 - sg))).astype(BF16)
         grads[these, ff : 2 * ff] = (dh * act).astype(BF16)
         grads[these, 2 * ff :] = hidden
+        pltpu.make_async_copy(grads.at[these], out_grads.at[these], out_sem.at[total + 1]).start()
         return carry
 
     lax.fori_loop(0, PLANE, point, 0)
     dp_out = pltpu.make_async_copy(dp, out_dp, out_sem.at[total + 2])
-    wide_out(1).start()
     dp_out.start()
 
     for n in range(3):
@@ -879,7 +879,7 @@
         dst[...] = src[...]
 
 
-def hand_over(*arrays, steps=4):
+def hand_over(*arrays, steps=2):
     specs = []
     for array in arrays:
         count = array.shape[0]

time: 222 us -> 219 us (0.986)
  no operation moved by 1% of the time
where the time goes in v4:
time: 219 us
  Pallas kernels  219 us (100%)
    pallas_call x1, Pallas kernels, dispatch(): pl.pallas_call(functools.partial(dispatch_kernel, width, chunks), out_sha...  133 us
    pallas_call x1, Pallas kernels, combine(): pl.pallas_call(functools.partial(combine_kernel, width, chunks), out_shap...  82.1 us

profile of v4, /device:TPU:32, one launch (start us, length us, event | category | flops | bytes accessed | tf_op | source)
XLA Modules:
  0.0 219.2 jit_solution(15496302808577084169)
XLA Ops:
  0.6 133.5 %dispatch.1 = (bf16[16,8,144,256]{3,2,1,0:T(8,128)(2,1)}, bf16[2048,768]{1,0:T(8,128)(2,1)}, bf16[1152,1152]{1,0:T(8,128)(2,1)}, f32[8,8,128]{2,1,0:T(8,128)}, f32[8,1024]{1,0:T(8,128)}) custom-call(bf16[128,2048]{1,0:T(8,128)(2,1)} %tok.1, bf16[128,2048]{1,0:T(8,128)(2,1)} %cot.1, s32[8,128]{1,0:T(8,128)} %bitcast.12, bf16[8,128]{1,0:T(8,128)(2,1)} %bitcast.14, ...), custom_call_target="tpu_custom_call" | custom-call | tf_op jit(solution)/shard_map/dispatch/pallas_call | solution.py:447
  134.1 82.1 %combine.1 = (bf16[128,2048]{1,0:T(8,128)(2,1)}, bf16[8,128]{1,0:T(8,128)(2,1)}, f32[512,384]{1,0:T(8,128)}, f32[512,384]{1,0:T(8,128)}, f32[384,512]{1,0:T(8,128)}) custom-call(bf16[16,8,144,256]{3,2,1,0:T(8,128)(2,1)} %get-tuple-element.20.rows_in, bf16[2048,768]{1,0:T(8,128)(2,1)} %get-tuple-element.21.wide_in, ...), custom_call_target="tpu_custom_call" | custom-call | tf_op jit(solution)/shard_map/combine/pallas_call | solution.py:820
  216.2 3.0 %hand_over.1 = (bf16[128,2048]{1,0:T(8,128)(2,1)}, bf16[8,128]{1,0:T(8,128)(2,1)}, f32[512,384]{1,0:T(8,128)}, f32[512,384]{1,0:T(8,128)}, f32[384,512]{1,0:T(8,128)}) custom-call(bf16[128,2048]{1,0:T(8,128)(2,1)} %get-tuple-element.25.refs_0_, bf16[8,128]{1,0:T(8,128)(2,1)} %get-tuple-element.26.refs_1_, f32[512,384]{1,0:T(8,128)} %get-tuple-element.27.refs_2_, ...), custom_call_target="tpu_custom_call" | custom-call | tf_op jit(solution)/shard_map/hand_over/pallas_call | solution.py:890
